TPU v7x, 256 devices: a whole 4x4x8 slice. The times are simulated.
256 devices in a mesh: gx: 4 (over x), gy: 8 (over z_lo, core), gz: 8 (over z_hi, y).
Axes of the slice: x: 4, y: 4, z: 8 (z_hi: 2, z_lo: 4; z = z_hi * 4 + z_lo), core: 2. Of those that a mesh axis runs over, the one named last changes fastest.
Arguments:
- features: bfloat16 [32, 32, 256, 1024], P(None, 'gx', 'gy', 'gz'), may hold values from -12 to 12
- posteriors: bfloat16 [16, 32, 256, 1024], P(None, 'gx', 'gy', 'gz'), may hold values from 0 to 1, as said below
Outputs:
- segmentation: bfloat16 [16, 32, 256, 1024], P(None, 'gx', 'gy', 'gz')
- class_means: float32 [16, 32], replicated
Inputs may be any that keep to these rules, and one draw needn't show every extreme that they name: Each voxel's 16 initial posteriors are positive and sum to one up to rounding.
All inputs are finite; a program needn't handle non-finite values.
Results may differ from a plain program's by a relative error of at most 0.0075.
Values may be sent and summed in bfloat16 or wider, within the bound.
A program may use at most 128 MiB of HBM per device.

v0:
```python
import jax
import jax.numpy as jnp
from jax import lax
from jax.sharding import PartitionSpec as P

SWEEPS = 2


beta_coupling = 1.0
ridge = 0.1


def with_halo(x, sides, width):
    for axis, dim in sides:
        count, length = (lax.axis_size(axis), x.shape[dim])
        up = [(i, (i + 1) % count) for i in range(count - 1)]
        down = [(j, i) for i, j in up]
        last = lax.slice_in_dim(x, length - width, length, axis=dim)
        initial = lax.slice_in_dim(x, 0, width, axis=dim)
        before = lax.ppermute(last, axis, up)
        after = lax.ppermute(initial, axis, down)
        x = jnp.concatenate([before, x, after], axis=dim)
    return x


def finish(counts, total_weight, first_moment, scatter):
    identity = jnp.eye(first_moment.shape[1], dtype=jnp.float32)
    centers = first_moment / counts[:, None]
    spread = (
        scatter / counts[:, None, None]
        - centers[:, :, None] * centers[:, None, :]
        + ridge * identity
    )
    factor = jnp.linalg.cholesky(spread)
    whiten = jax.vmap(
        lambda lower_factor: jax.scipy.linalg.solve_triangular(lower_factor, identity, lower=True)
    )(factor)
    offset = jnp.einsum("kgf,kf->kg", whiten, centers, precision=lax.Precision.HIGHEST)
    biases = jnp.log(counts / total_weight) - jnp.sum(
        jnp.log(jnp.diagonal(factor, axis1=1, axis2=2)), axis=1
    )
    return (centers, whiten, offset, biases)


def local_moments(posterior, voxels):
    flat_post = posterior.reshape(posterior.shape[0], -1)
    flat_vox = voxels.reshape(voxels.shape[0], -1)
    contract = (((1,), (1,)), ((), ()))
    counts = jnp.sum(flat_post.astype(jnp.float32), axis=1)
    first_moment = lax.dot_general(
        flat_post, flat_vox, contract, preferred_element_type=jnp.float32
    )

    def second(weights_row):
        weighted = weights_row[None, :] * flat_vox
        return lax.dot_general(weighted, flat_vox, contract, preferred_element_type=jnp.float32)

    scatter = lax.map(second, flat_post)
    return (counts, first_moment, scatter)


def fit(posterior, voxels):
    counts, first_moment, scatter = local_moments(posterior, voxels)
    counts, first_moment, scatter = lax.psum((counts, first_moment, scatter), ("gx", "gy", "gz"))
    return finish(counts, jnp.sum(counts), first_moment, scatter)


def loglik(voxels, whiten, offset, biases):
    flat_vox = voxels.reshape(voxels.shape[0], -1)
    rounded = whiten.astype(jnp.bfloat16)

    def per_class(class_record):
        matrix, shift, level = class_record
        whitened = jnp.dot(matrix, flat_vox, preferred_element_type=jnp.float32) - shift[:, None]
        return level - 0.5 * jnp.sum(whitened * whitened, axis=0)

    scores = lax.map(per_class, (rounded, offset, biases))
    return scores.reshape((whiten.shape[0],) + voxels.shape[1:])


def neighbours(padded):
    inner = padded[:, 2:, 1:-1, 1:-1] + padded[:, :-2, 1:-1, 1:-1]
    inner = inner + padded[:, 1:-1, 2:, 1:-1] + padded[:, 1:-1, :-2, 1:-1]
    return inner + padded[:, 1:-1, 1:-1, 2:] + padded[:, 1:-1, 1:-1, :-2]


def state_update(scores, near_sum):
    return jax.nn.softmax(scores + beta_coupling * near_sum, axis=0).astype(jnp.bfloat16)


def local(features, posteriors):
    centers, whiten, offset, biases = fit(posteriors, features)
    scores = loglik(features, whiten, offset, biases)
    current = posteriors
    for pass_index in range(SWEEPS):
        padded = with_halo(current, (("gx", 1), ("gy", 2), ("gz", 3)), 1)
        current = state_update(scores, neighbours(padded.astype(jnp.float32)))
    centers, whiten, offset, biases = fit(current, features)
    scores = loglik(features, whiten, offset, biases)
    padded = with_halo(current, (("gx", 1), ("gy", 2), ("gz", 3)), 1)
    segmentation = state_update(scores, neighbours(padded.astype(jnp.float32)))
    return (segmentation, centers)


def solution(mesh):
    placed = (P(None, "gx", "gy", "gz"), P(None, "gx", "gy", "gz"))
    return jax.shard_map(
        local,
        mesh=mesh,
        in_specs=placed,
        out_specs=(P(None, "gx", "gy", "gz"), P()),
        check_vma=False,
    )
```

profile of v0, /device:TPU:1, one launch (start us, length us, event | category | flops | bytes accessed | tf_op | source)
XLA Modules:
  0.0 1122.7 jit_solution(12491573714184528234)
XLA Ops:
  7.2 4.4 copy.131
  12.3 53.4 %while.40 = (s32[]{:T(128)}, f32[16,32,32]{1,2,0:T(8,128)S(1)}, bf16[16,32768]{1,0:T(8,128)(2,1)S(1)}, bf16[32,32768]{1,0:T(8,128)(2,1)}, s32[]{:T(128)}) while((s32[]{:T(128)}, f32[16,32,32]{1,2,0:T(8,128)S(1)}, bf16[16,32768]{1,0:T(8,128)(2,1)S(1)}, bf16[32,32768]{1,0:T(8,128)(2,1)}, s32[]{:T(128)}) %tuple.99), condition=%wide.region_1.2_spmd, body=%wide.region_0.0_spmd.sunk | while | flops 68157440 | bytes 4407873 | solution.py:58
  66.5 4.0 collective-permute-start
  71.8 3.6 fusion.38
  75.7 81.9 %all-reduce.1 = (f32[16,32]{1,0:T(8,128)S(1)}, f32[16]{0:T(128)S(1)}) all-reduce(f32[16,32]{1,0:T(8,128)S(1)} %fusion.38, f32[16]{0:T(128)S(1)} %convert_reduce_fusion.1), channel_id=1, replica_groups=mesh['gx'=4,'gy'=8,'gz'=8] {'gx','gy','gz'}, use_global_device_ids=true, to_apply=%region_5.6 | all-reduce | flops 528 | bytes 4224 | tf_op jit(solution)/shard_map/psum | solution.py:64
  158.4 161.3 %all-reduce.5.cloned.1.call-done = f32[16,32,32]{1,2,0:T(8,128)} async-done(((f32[16,32,32]{1,2,0:T(8,128)}), f32[16,32,32]{1,2,0:T(8,128)}) %all-reduce.5.cloned.1.call-update) | async-done | bytes 65552 | tf_op jit(solution)/shard_map/psum | solution.py:64
  322.0 46.9 %custom-call.12 = f32[16,32,32]{2,1,0:T(8,128)S(1)} custom-call(f32[16,32,32]{2,1,0:T(8,128)S(1)} %fusion.51), custom_call_target="Cholesky" | custom-call | tf_op jit(solution)/shard_map/jit(cholesky)/cholesky | solution.py:34
  369.2 39.4 %custom-call.13 = f32[16,1,32,32]{2,3,1,0:T(8,128)S(1)} custom-call(f32[16,1,32,32]{3,2,1,0:T(8,128)S(1)} %get-tuple-element.172), custom_call_target="InvertDiagBlocksLowerTriangular" | custom-call | tf_op jit(solution)/shard_map/vmap(jit(_solve_triangular))/triangular_solve | solution.py:36
  423.5 4.1 collective-permute-start.4
  431.0 75.4 %while.41 = (s32[]{:T(128)}, f32[16,32768]{1,0:T(8,128)S(1)}, f32[16]{0:T(128)S(1)}, bf16[16,32,32]{2,1,0:T(8,128)(2,1)S(1)}, bf16[32,32768]{1,0:T(8,128)(2,1)}, /*index=5*/f32[16,32]{1,0:T(8,128)S(1)}, s32[]{:T(128)}, s32[]{:T(128)}) while((s32[]{:T(128)}, f32[16,32768]{1,0:T(8,128)S(1)}, f32[16]{0:T(128)S(1)}, ...), condition=%wide.region_12.15_spmd, body=%wide.region_10.14_spmd.sunk | while | flops 70287360 | bytes 2761585 | solution.py:77
  515.5 5.0 maximum_convert_fusion
  529.2 3.9 collective-permute-done.7
  533.3 3.6 collective-permute-start.8
  538.9 3.8 collective-permute-done.9
  549.0 4.7 collective-permute-start.10
  564.5 5.6 maximum_convert_fusion.1
  582.2 53.2 %while.42 = (s32[]{:T(128)}, f32[16,32,32]{1,2,0:T(8,128)S(1)}, bf16[16,32768]{1,0:T(8,128)(2,1)S(1)}, bf16[32,32768]{1,0:T(8,128)(2,1)}, s32[]{:T(128)}) while((s32[]{:T(128)}, f32[16,32,32]{1,2,0:T(8,128)S(1)}, bf16[16,32768]{1,0:T(8,128)(2,1)S(1)}, bf16[32,32768]{1,0:T(8,128)(2,1)}, s32[]{:T(128)}) %tuple.101), condition=%wide.region_18.21_spmd, body=%wide.region_17.20_spmd.sunk | while | flops 68157440 | bytes 4407873 | solution.py:58
  636.2 89.4 %all-reduce = (f32[16,32]{1,0:T(8,128)S(1)}, f32[16]{0:T(128)S(1)}) all-reduce(f32[16,32]{1,0:T(8,128)S(1)} %fusion.41, f32[16]{0:T(128)S(1)} %get-tuple-element.166), channel_id=1, replica_groups=mesh['gx'=4,'gy'=8,'gz'=8] {'gx','gy','gz'}, use_global_device_ids=true, to_apply=%region_22.25 | all-reduce | flops 528 | bytes 4224 | tf_op jit(solution)/shard_map/psum | solution.py:64
  726.3 170.8 %all-reduce.7.cloned.1.call-done = f32[16,32,32]{1,2,0:T(8,128)} async-done(((f32[16,32,32]{1,2,0:T(8,128)}), f32[16,32,32]{1,2,0:T(8,128)}) %all-reduce.7.cloned.1.call-update) | async-done | bytes 65552 | tf_op jit(solution)/shard_map/psum | solution.py:64
  899.4 46.9 %custom-call.14 = f32[16,32,32]{2,1,0:T(8,128)S(1)} custom-call(f32[16,32,32]{2,1,0:T(8,128)S(1)} %fusion.48), custom_call_target="Cholesky" | custom-call | tf_op jit(solution)/shard_map/jit(cholesky)/cholesky | solution.py:34
  946.6 39.4 %custom-call.15 = f32[16,1,32,32]{2,3,1,0:T(8,128)S(1)} custom-call(f32[16,1,32,32]{3,2,1,0:T(8,128)S(1)} %get-tuple-element.164), custom_call_target="InvertDiagBlocksLowerTriangular" | custom-call | tf_op jit(solution)/shard_map/vmap(jit(_solve_triangular))/triangular_solve | solution.py:36
  1004.7 3.6 collective-permute-start.16
  1011.9 86.8 %while.43 = (s32[]{:T(128)}, f32[16,32768]{1,0:T(8,128)S(1)}, f32[16]{0:T(128)S(1)}, bf16[16,32,32]{2,1,0:T(8,128)(2,1)}, bf16[32,32768]{1,0:T(8,128)(2,1)}, /*index=5*/f32[16,32]{1,0:T(8,128)}, s32[]{:T(128)}, s32[]{:T(128)}) while((s32[]{:T(128)}, f32[16,32768]{1,0:T(8,128)S(1)}, f32[16]{0:T(128)S(1)}, bf16[16,32,32]{2,1,0:T(8,128)(2,1)}, ...), condition=%wide.region_27.30_spmd, body=%wide.region_25.29_spmd.sunk | while | flops 70287360 | bytes 2761709 | solution.py:77
  1105.4 5.4 maximum_convert_fusion.2
  (381 shorter events, 378.5 us)
Async XLA Ops:
  7.2 312.5 %all-reduce.5.cloned.1.call-start = ((), (), s32[]{:S(2)}) async-start(), calls=%async_computation | async-start | bytes 524288 | tf_op jit(solution)/shard_map/psum | solution.py:64
  66.4 830.7 %all-reduce.7.cloned.1.call-start = ((), (), s32[]{:S(2)}) async-start(), calls=%async_computation.1 | async-start | bytes 524288 | tf_op jit(solution)/shard_map/psum | solution.py:64
  66.5 344.3 %collective-permute-start = (bf16[16,1,32,128]{3,2,1,0:T(8,128)(2,1)S(1)}, bf16[16,1,32,128]{3,2,1,0:T(8,128)(2,1)S(1)}, u32[]{:S(2)}, u32[]{:S(2)}) collective-permute-start(bf16[16,1,32,128]{3,2,1,0:T(8,128)(2,1)S(1)} %get-tuple-element.191), channel_id=1, source_target_pairs={{0,64},{64,128},{128,192},{1,65},{65,129},{129,193},{2,66},{66,130... | collective-permute-start | bytes 393224 | tf_op jit(solution)/shard_map/ppermute | solution.py:20
  70.5 340.5 %collective-permute-start.1 = (bf16[16,1,32,128]{3,2,1,0:T(8,128)(2,1)S(1)}, bf16[16,1,32,128]{3,2,1,0:T(8,128)(2,1)S(1)}, u32[]{:S(2)}, u32[]{:S(2)}) collective-permute-start(bf16[16,1,32,128]{3,2,1,0:T(8,128)(2,1)S(1)} %get-tuple-element.190), channel_id=1, source_target_pairs={{64,0},{128,64},{192,128},{65,1},{129,65},{193,129},{66,2},{130,66... | collective-permute-start | bytes 393224 | tf_op jit(solution)/shard_map/ppermute | solution.py:21
  75.6 334.1 %copy-start.8 = (f32[32,32]{0,1:T(8,128)}, f32[32,32]{0,1:T(8,128)S(1)}, u32[]{:S(2)}) copy-start(f32[32,32]{0,1:T(8,128)S(1)} %fusion.55) | copy-start | bytes 12292
  75.7 334.3 %copy-start.19 = (pred[32,32]{1,0:T(8,128)(4,1)}, pred[32,32]{1,0:T(8,128)(4,1)S(1)}, u32[]{:S(2)}) copy-start(pred[32,32]{1,0:T(8,128)(4,1)S(1)} %iota_compare_fusion) | copy-start | bytes 3076
  411.1 6.4 collective-permute-start.2
  414.1 5.8 collective-permute-start.3
  423.5 86.2 %collective-permute-start.4 = (bf16[16,10,34,1]{2,0,3,1:T(8,128)(2,1)S(1)}, bf16[16,10,34,1]{2,0,3,1:T(8,128)(2,1)}, u32[]{:S(2)}, u32[]{:S(2)}) collective-permute-start(bf16[16,10,34,1]{2,0,3,1:T(8,128)(2,1)S(1)} %copy.69), channel_id=1, source_target_pairs={{0,1},{1,2},{2,3},{3,4},{4,5},{5,6},{6,7},{8,9},{9,10},{10,11},{11... | collective-permute-start | bytes 32648 | tf_op jit(solution)/shard_map/ppermute | solution.py:20
  429.5 83.1 %collective-permute-start.5 = (bf16[16,10,34,1]{2,0,3,1:T(8,128)(2,1)}, bf16[16,10,34,1]{2,0,3,1:T(8,128)(2,1)}, u32[]{:S(2)}, u32[]{:S(2)}) collective-permute-start(bf16[16,10,34,1]{2,0,3,1:T(8,128)(2,1)} %copy.70), channel_id=1, source_target_pairs={{1,0},{2,1},{3,2},{4,3},{5,4},{6,5},{7,6},{9,8},{10,9},{11,10},{12... | collective-permute-start | bytes 32648 | tf_op jit(solution)/shard_map/ppermute | solution.py:21
  524.4 4.8 collective-permute-start.6
  527.3 5.8 collective-permute-start.7
  533.3 5.6 collective-permute-start.8
  536.9 5.8 collective-permute-start.9
  549.0 9.0 collective-permute-start.10
  556.6 5.1 collective-permute-start.11
  577.2 412.2 %collective-permute-start.12 = (bf16[16,1,32,128]{3,2,1,0:T(8,128)(2,1)S(1)}, bf16[16,1,32,128]{3,2,1,0:T(8,128)(2,1)S(1)}, u32[]{:S(2)}, u32[]{:S(2)}) collective-permute-start(bf16[16,1,32,128]{3,2,1,0:T(8,128)(2,1)S(1)} %get-tuple-element.186), channel_id=1, source_target_pairs={{0,64},{64,128},{128,192},{1,65},{65,129},{129,193},{2,66},{66,130... | collective-permute-start | bytes 393224 | tf_op jit(solution)/shard_map/ppermute | solution.py:20
  580.2 409.2 %collective-permute-start.13 = (bf16[16,1,32,128]{3,2,1,0:T(8,128)(2,1)S(1)}, bf16[16,1,32,128]{3,2,1,0:T(8,128)(2,1)S(1)}, u32[]{:S(2)}, u32[]{:S(2)}) collective-permute-start(bf16[16,1,32,128]{3,2,1,0:T(8,128)(2,1)S(1)} %get-tuple-element.187), channel_id=1, source_target_pairs={{64,0},{128,64},{192,128},{65,1},{129,65},{193,129},{66,2},{130,66... | collective-permute-start | bytes 393224 | tf_op jit(solution)/shard_map/ppermute | solution.py:21
  582.2 314.8 %copy-start.9 = (f32[32,32]{0,1:T(8,128)S(1)}, f32[32,32]{0,1:T(8,128)}, u32[]{:S(2)}) copy-start(f32[32,32]{0,1:T(8,128)} %copy-done.8) | copy-start | bytes 12292
  635.5 350.5 %copy-start.18 = (f32[32,32]{1,0:T(8,128)S(1)}, f32[32,32]{1,0:T(8,128)}, u32[]{:S(2)}) copy-start(f32[32,32]{1,0:T(8,128)} %copy-done.17) | copy-start | bytes 12292
  989.6 5.8 collective-permute-start.14
  992.5 5.8 collective-permute-start.15
  1004.7 95.8 %collective-permute-start.16 = (bf16[16,10,34,1]{2,0,3,1:T(8,128)(2,1)}, bf16[16,10,34,1]{2,0,3,1:T(8,128)(2,1)}, u32[]{:S(2)}, u32[]{:S(2)}) collective-permute-start(bf16[16,10,34,1]{2,0,3,1:T(8,128)(2,1)} %copy.84), channel_id=1, source_target_pairs={{0,1},{1,2},{2,3},{3,4},{4,5},{5,6},{6,7},{8,9},{9,10},{10,11},{11... | collective-permute-start | bytes 32648 | tf_op jit(solution)/shard_map/ppermute | solution.py:20
  1010.2 92.3 %collective-permute-start.17 = (bf16[16,10,34,1]{2,0,3,1:T(8,128)(2,1)}, bf16[16,10,34,1]{2,0,3,1:T(8,128)(2,1)}, u32[]{:S(2)}, u32[]{:S(2)}) collective-permute-start(bf16[16,10,34,1]{2,0,3,1:T(8,128)(2,1)} %copy.85), channel_id=1, source_target_pairs={{1,0},{2,1},{3,2},{4,3},{5,4},{6,5},{7,6},{9,8},{10,9},{11,10},{12... | collective-permute-start | bytes 32648 | tf_op jit(solution)/shard_map/ppermute | solution.py:21
  (18 other events, 876.5 us)
Sparse Core Ops, SparseCore 0:
  66.5 253.0 all-reduce.4
  636.3 260.7 all-reduce.6
where the time goes:
time: 1140 us; the launch traced here: 1120 us
  waiting for transfers between devices  346 us (30%)
  other arithmetic  233 us (20%)
  matrix products  182 us (16%)
  blocking collectives  171 us (15%)
  local copies, waits for them, and re-layouts  127 us (11%)
  starting transfers between devices  46.3 us (4%)
  between operations  15 us (1%)
    psum x2, waiting for transfers between devices, fit(): lax.psum((counts, first_moment, scatter), ('gx', 'gy', 'gz'))  332 us
    psum x2, blocking collectives, fit(): lax.psum((counts, first_moment, scatter), ('gx', 'gy', 'gz'))  171 us
    another operation x7, other arithmetic, finish(): factor = jnp.linalg.cholesky(spread)  94.1 us
    dot_general x32, matrix products, second(): lax.dot_general(weighted, flat_vox, contract, preferred_element_type=jnp....  93.1 us
    dot_general x32, matrix products, per_class(): jnp.dot(matrix, flat_vox, preferred_element_type=jnp.float32)  79.2 us
    another operation x4, other arithmetic, finish(): jax.scipy.linalg.solve_triangular(lower_factor, identity, lower=True)  79 us
    ppermute x9, starting transfers between devices, with_halo(): before = lax.ppermute(last, axis, up)  31.8 us
    dynamic_update_slice x32, local copies, waits for them, and re-layouts, loglik(): scores = lax.map(per_class, (rounded, offset, biases))  30.3 us
  transfers between devices with their start and end apart: 20, of which 8 were waited for; matrix products, arithmetic and copies ran while one was open for 38% of the time, Pallas kernels for 0%

commit v1 on v0

v1 whole, which is shorter than its diff:
```python
import functools

import jax
import jax.numpy as jnp
from jax import lax
from jax.experimental import pallas as pl
from jax.experimental.pallas import tpu as pltpu
from jax.sharding import PartitionSpec as P

SWEEPS = 2
FEATS = 32
CLASSES = 16
LANES = 128
GROUP = 8
PIECES = 8
PIECE_ROWS = 24
AUG = 48

beta_coupling = 1.0
ridge = 0.1

AXES = ("gx", "gy", "gz")
MESH = pl.DeviceIdType.MESH
VMEM = pl.BlockSpec(memory_space=pltpu.VMEM)
NT = (((1,), (1,)), ((), ()))


def augmented(rows):
    count = rows.shape[1]
    index = lax.broadcasted_iota(jnp.int32, (AUG - FEATS, count), 0)
    extra = jnp.where(index < 3, 1.0, 0.0).astype(jnp.bfloat16)
    return jnp.concatenate([rows, extra], axis=0)


def face_of(q_rows, low_ref, high_ref, step):
    side = lax.broadcasted_iota(jnp.int32, (16, LANES), 0)
    lane = lax.broadcasted_iota(jnp.int32, (16, LANES), 1)
    pick = ((side == 0) & (lane == 0)) | ((side == 1) & (lane == LANES - 1))
    pick = jnp.where(pick, 1.0, 0.0).astype(jnp.bfloat16)
    faces = lax.dot_general(pick, q_rows, NT, preferred_element_type=jnp.float32)
    width = GROUP * CLASSES
    where = pl.ds(pl.multiple_of(step * width, width), width)
    low_ref[:, where] = faces[0:1].astype(jnp.bfloat16)
    high_ref[:, where] = faces[1:2].astype(jnp.bfloat16)


def add_moments(rows, posts, total):
    weighted = []
    for row, post in zip(rows, posts):
        parts = [post[k : k + 1, :] * row for k in range(CLASSES)] + [post]
        weighted.append(jnp.concatenate(parts, axis=0))
    left = jnp.concatenate(weighted, axis=1)
    right = augmented(jnp.concatenate(rows, axis=1))
    total[:, :AUG] += lax.dot_general(left, right, NT, preferred_element_type=jnp.float32)


def pack_moments(total, out_ref):
    rows_per = FEATS // PIECES
    for piece in range(PIECES):
        blocks = []
        for r in range(rows_per):
            row = piece * rows_per + r
            blocks.append(total[pl.ds(row, CLASSES, stride=FEATS), :][:, :FEATS])
        out_ref[piece, :CLASSES, :] = jnp.concatenate(blocks, axis=1)
        if piece < 2:
            start = CLASSES * FEATS + 8 * piece
            out_ref[piece, CLASSES:, :] = total[start : start + 8, :]
        else:
            out_ref[piece, CLASSES:, :] = jnp.zeros((8, LANES), jnp.float32)


def moments_kernel(f_ref, q_ref, out_ref, low_ref, high_ref, total):
    count_x, count_y = q_ref.shape[0], q_ref.shape[1]
    per_x = count_y // GROUP
    total[...] = jnp.zeros_like(total)

    def step(c, carry):
        x, y = c // per_x, (c % per_x) * GROUP
        rows = [f_ref[x, y + g] for g in range(GROUP)]
        posts = [q_ref[x, y + g] for g in range(GROUP)]
        add_moments(rows, posts, total)
        face_of(jnp.concatenate(posts, axis=0), low_ref, high_ref, c)
        return carry

    lax.fori_loop(0, count_x * per_x, step, 0)
    pack_moments(total, out_ref)


def moments(f, q):
    faces = q.shape[0] * q.shape[1] * CLASSES
    return pl.pallas_call(
        moments_kernel,
        name="moments",
        out_shape=(
            jax.ShapeDtypeStruct((PIECES, PIECE_ROWS, LANES), jnp.float32),
            jax.ShapeDtypeStruct((1, faces), jnp.bfloat16),
            jax.ShapeDtypeStruct((1, faces), jnp.bfloat16),
        ),
        in_specs=[VMEM] * 2,
        out_specs=(VMEM,) * 3,
        scratch_shapes=[pltpu.VMEM((CLASSES * FEATS + CLASSES, LANES), jnp.float32)],
    )(f, q)


def sum_kernel(sizes, part_ref, out_ref, held_y, held_z, held_x, full, send, recv):
    me = {axis: lax.axis_index(axis) for axis in AXES}

    def partner(axis, d):
        return lax.rem(me[axis] + d, sizes[axis])

    barrier = pltpu.get_barrier_semaphore()
    for axis in AXES:
        for d in range(1, sizes[axis]):
            pl.semaphore_signal(
                barrier, inc=1, device_id={axis: partner(axis, d)}, device_id_type=MESH
            )
    pl.semaphore_wait(barrier, sum(sizes[axis] - 1 for axis in AXES))

    def exchange(stage, axis, source, held):
        copies = []
        for d in range(1, sizes[axis]):
            there = partner(axis, d)
            copies.append(
                pltpu.make_async_remote_copy(
                    src_ref=source(there),
                    dst_ref=held.at[me[axis]],
                    send_sem=send.at[stage, d],
                    recv_sem=recv.at[stage, d],
                    device_id={axis: there},
                    device_id_type=MESH,
                )
            )
        for copy in copies:
            copy.start()
        for copy in copies:
            copy.wait()

    def added(held, count):
        value = held[0]
        for i in range(1, count):
            value = value + held[i]
        return value

    y, z, x = me["gy"], me["gz"], me["gx"]
    group = PIECES // sizes["gy"]
    held_y[y] = part_ref[pl.ds(y * group, group)]
    exchange(0, "gy", lambda there: part_ref.at[pl.ds(there * group, group)], held_y)
    held_z[z] = added(held_y, sizes["gy"])
    exchange(1, "gz", lambda there: held_z.at[z], held_z)
    held_x[x] = added(held_z, sizes["gz"])
    exchange(2, "gx", lambda there: held_x.at[x], held_x)
    full[y] = added(held_x, sizes["gx"])
    exchange(3, "gy", lambda there: full.at[y], full)
    for i in range(sizes["gy"]):
        out_ref[pl.ds(i * group, group)] = full[i]


def summed(part):
    sizes = {axis: lax.axis_size(axis) for axis in AXES}
    most = max(sizes.values())
    block = (PIECES // sizes["gy"], PIECE_ROWS, LANES)
    return pl.pallas_call(
        functools.partial(sum_kernel, sizes),
        name="sum_over_devices",
        out_shape=jax.ShapeDtypeStruct(part.shape, jnp.float32),
        in_specs=[VMEM],
        out_specs=VMEM,
        scratch_shapes=[
            pltpu.VMEM((sizes["gy"],) + block, jnp.float32),
            pltpu.VMEM((sizes["gz"],) + block, jnp.float32),
            pltpu.VMEM((sizes["gx"],) + block, jnp.float32),
            pltpu.VMEM((sizes["gy"],) + block, jnp.float32),
            pltpu.SemaphoreType.DMA((4, most)),
            pltpu.SemaphoreType.DMA((4, most)),
        ],
        compiler_params=pltpu.CompilerParams(collective_id=0, has_side_effects=True),
    )(part)


def finish_kernel(sum_ref, matrix_ref, bias_ref, mean_ref):
    last = jnp.concatenate([sum_ref[0, CLASSES:, :], sum_ref[1, CLASSES:, :]], axis=0)
    counts = last[:, FEATS : FEATS + 1]
    mean = last[:, :FEATS] / counts
    mean_ref[...] = mean
    total_weight = jnp.sum(counts, axis=0, keepdims=True)
    lane = lax.broadcasted_iota(jnp.int32, (CLASSES, LANES), 1)
    small = lax.broadcasted_iota(jnp.int32, (CLASSES, FEATS), 1)
    rows_per = FEATS // PIECES
    rows = []
    for i in range(FEATS):
        start = (i % rows_per) * FEATS
        second = sum_ref[i // rows_per, :CLASSES, start : start + FEATS]
        spread = second / counts - mean[:, i : i + 1] * mean + jnp.where(small == i, ridge, 0.0)
        unit = jnp.where(small == i, 1.0, 0.0)
        shift = jnp.where(small == 0, mean[:, i : i + 1], 0.0)
        rows.append(jnp.concatenate([unit, shift, spread, jnp.zeros_like(spread)], axis=1))
    diagonal = jnp.ones((CLASSES, LANES), jnp.float32)
    for k in range(FEATS):
        pivot = jnp.sqrt(rows[k][:, 64 + k : 65 + k])
        diagonal = jnp.where(lane == k, pivot, diagonal)
        row = rows[k] * (1.0 / pivot)
        rows[k] = row
        for i in range(k + 1, FEATS):
            rows[i] = rows[i] - row[:, 64 + i : 65 + i] * row
    logdet = jnp.sum(jnp.log(diagonal), axis=1, keepdims=True)
    bias_ref[...] = jnp.broadcast_to(jnp.log(counts / total_weight) - logdet, (CLASSES, LANES))
    for g in range(FEATS):
        offset = -rows[g][:, FEATS : FEATS + 1]
        high = offset.astype(jnp.bfloat16).astype(jnp.float32)
        middle = (offset - high).astype(jnp.bfloat16).astype(jnp.float32)
        low = offset - high - middle
        tail = jnp.where(lane == 34, low, 0.0)
        tail = jnp.where(lane == 33, middle, tail)
        tail = jnp.where(lane == 32, high, tail)
        value = jnp.where(lane < FEATS, rows[g], tail)
        matrix_ref[g * CLASSES : (g + 1) * CLASSES, :] = value.astype(jnp.bfloat16)


def finish(total):
    return pl.pallas_call(
        finish_kernel,
        name="finish",
        out_shape=(
            jax.ShapeDtypeStruct((FEATS * CLASSES, LANES), jnp.bfloat16),
            jax.ShapeDtypeStruct((CLASSES, LANES), jnp.float32),
            jax.ShapeDtypeStruct((CLASSES, FEATS), jnp.float32),
        ),
        in_specs=[VMEM],
        out_specs=(VMEM,) * 3,
    )(total)


def fill_padded(padded, q_ref, xlo_ref, xhi_ref, ylo_ref, yhi_ref):
    count_x, count_y = q_ref.shape[0], q_ref.shape[1]
    padded[0, 1 : count_y + 1] = xlo_ref[...]
    padded[count_x + 1, 1 : count_y + 1] = xhi_ref[...]
    for x in range(count_x):
        padded[x + 1, 1 : count_y + 1] = q_ref[x]
        padded[x + 1, 0] = ylo_ref[x]
        padded[x + 1, count_y + 1] = yhi_ref[x]


def near_of(padded, zlo_ref, zhi_ref, x, y, c):
    flat = (GROUP * CLASSES, LANES)

    def block(dx, dy):
        return padded[x + 1 + dx, pl.ds(y + 1 + dy, GROUP)].reshape(flat)

    total = block(1, 0).astype(jnp.float32) + block(-1, 0).astype(jnp.float32)
    total = total + block(0, 1).astype(jnp.float32) + block(0, -1).astype(jnp.float32)
    a = lax.broadcasted_iota(jnp.int32, (LANES, LANES), 0)
    b = lax.broadcasted_iota(jnp.int32, (LANES, LANES), 1)
    beside = jnp.where((a == b + 1) | (a + 1 == b), 1.0, 0.0).astype(jnp.bfloat16)
    total = total + jnp.dot(block(0, 0), beside, preferred_element_type=jnp.float32)
    width = GROUP * CLASSES
    where = pl.ds(pl.multiple_of(c * width, width), width)
    side = lax.broadcasted_iota(jnp.int32, (8, width), 0)
    low = jnp.broadcast_to(zlo_ref[:, where].astype(jnp.float32), (8, width))
    high = jnp.broadcast_to(zhi_ref[:, where].astype(jnp.float32), (8, width))
    column = jnp.transpose(jnp.where(side == 0, low, high))
    lane = lax.broadcasted_iota(jnp.int32, flat, 1)
    edge = jnp.where(lane == LANES - 1, column[:, 1:2], 0.0)
    return total + jnp.where(lane == 0, column[:, 0:1], edge)


def update(scores, near):
    value = (scores + beta_coupling * near).reshape(GROUP, CLASSES, LANES)
    value = jnp.exp(value - jnp.max(value, axis=1, keepdims=True))
    value = value * (1.0 / jnp.sum(value, axis=1, keepdims=True))
    return value.astype(jnp.bfloat16)


def scores_of(f_ref, matrix_ref, bias_ref, x, y):
    bias = bias_ref[...]
    parts = []
    for g in range(0, GROUP, 2):
        pair = jnp.concatenate([f_ref[x, y + g], f_ref[x, y + g + 1]], axis=1)
        pair = augmented(pair)
        total = None
        for m in range(0, FEATS * CLASSES, 128):
            white = jnp.dot(
                matrix_ref[m : m + 128, :AUG], pair, preferred_element_type=jnp.float32
            )
            square = jnp.sum((white * white).reshape(128 // CLASSES, CLASSES, 2 * LANES), axis=0)
            total = square if total is None else total + square
        parts.append(bias - 0.5 * total[:, :LANES])
        parts.append(bias - 0.5 * total[:, LANES:])
    return jnp.concatenate(parts, axis=0)


def first_kernel(f_ref, m_ref, b_ref, q_ref, xlo, xhi, ylo, yhi, zlo, zhi,
                 out_ref, scores_ref, low_ref, high_ref, padded):
    count_x, count_y = q_ref.shape[0], q_ref.shape[1]
    per_x = count_y // GROUP
    fill_padded(padded, q_ref, xlo, xhi, ylo, yhi)

    def step(c, carry):
        x, y = c // per_x, (c % per_x) * GROUP
        scores = scores_of(f_ref, m_ref, b_ref, x, y)
        scores_ref[x, pl.ds(y, GROUP)] = scores.reshape(GROUP, CLASSES, LANES)
        q = update(scores, near_of(padded, zlo, zhi, x, y, c))
        out_ref[x, pl.ds(y, GROUP)] = q
        face_of(q.reshape(GROUP * CLASSES, LANES), low_ref, high_ref, c)
        return carry

    lax.fori_loop(0, count_x * per_x, step, 0)


def second_kernel(f_ref, scores_ref, q_ref, xlo, xhi, ylo, yhi, zlo, zhi,
                  out_ref, sum_ref, low_ref, high_ref, padded, total):
    count_x, count_y = q_ref.shape[0], q_ref.shape[1]
    per_x = count_y // GROUP
    fill_padded(padded, q_ref, xlo, xhi, ylo, yhi)
    total[...] = jnp.zeros_like(total)

    def step(c, carry):
        x, y = c // per_x, (c % per_x) * GROUP
        scores = scores_ref[x, pl.ds(y, GROUP)].reshape(GROUP * CLASSES, LANES)
        q = update(scores, near_of(padded, zlo, zhi, x, y, c))
        out_ref[x, pl.ds(y, GROUP)] = q
        rows = [f_ref[x, y + g] for g in range(GROUP)]
        add_moments(rows, [q[g] for g in range(GROUP)], total)
        face_of(q.reshape(GROUP * CLASSES, LANES), low_ref, high_ref, c)
        return carry

    lax.fori_loop(0, count_x * per_x, step, 0)
    pack_moments(total, sum_ref)


def last_kernel(f_ref, m_ref, b_ref, q_ref, xlo, xhi, ylo, yhi, zlo, zhi, out_ref, padded):
    count_x, count_y = q_ref.shape[0], q_ref.shape[1]
    per_x = count_y // GROUP
    fill_padded(padded, q_ref, xlo, xhi, ylo, yhi)

    def step(c, carry):
        x, y = c // per_x, (c % per_x) * GROUP
        scores = scores_of(f_ref, m_ref, b_ref, x, y)
        out_ref[x, pl.ds(y, GROUP)] = update(scores, near_of(padded, zlo, zhi, x, y, c))
        return carry

    lax.fori_loop(0, count_x * per_x, step, 0)


def sweep_call(kernel, name, operands, q, out_shape, scratch=()):
    count_x, count_y = q.shape[0], q.shape[1]
    padded = pltpu.VMEM((count_x + 2, count_y + 2, CLASSES, LANES), jnp.bfloat16)
    return pl.pallas_call(
        kernel,
        name=name,
        out_shape=out_shape,
        in_specs=[VMEM] * len(operands),
        out_specs=jax.tree.map(lambda _: VMEM, out_shape),
        scratch_shapes=[padded] + list(scratch),
    )(*operands)


def halo_of(q, low, high):
    faces = {"gx": (q[0], q[-1]), "gy": (q[:, 0], q[:, -1]), "gz": (low, high)}
    got = []
    for axis, (first, last) in faces.items():
        count = lax.axis_size(axis)
        up = [(i, i + 1) for i in range(count - 1)]
        down = [(j, i) for i, j in up]
        got.append(lax.ppermute(last, axis, up))
        got.append(lax.ppermute(first, axis, down))
    return got


def local(features, posteriors):
    f = features.transpose(1, 2, 0, 3)
    q = posteriors.transpose(1, 2, 0, 3)
    face = jax.ShapeDtypeStruct((1, q.shape[0] * q.shape[1] * CLASSES), jnp.bfloat16)
    state = jax.ShapeDtypeStruct(q.shape, jnp.bfloat16)
    scores_shape = jax.ShapeDtypeStruct(q.shape, jnp.float32)
    sums = jax.ShapeDtypeStruct((PIECES, PIECE_ROWS, LANES), jnp.float32)
    total = pltpu.VMEM((CLASSES * FEATS + CLASSES, LANES), jnp.float32)

    part, low, high = moments(f, q)
    halo = halo_of(q, low, high)
    matrix, bias, _ = finish(summed(part))
    q, scores, low, high = sweep_call(
        first_kernel, "first_sweep", [f, matrix, bias, q] + halo, q,
        (state, scores_shape, face, face))
    halo = halo_of(q, low, high)
    q, part, low, high = sweep_call(
        second_kernel, "second_sweep", [f, scores, q] + halo, q,
        (state, sums, face, face), [total])
    halo = halo_of(q, low, high)
    matrix, bias, mean = finish(summed(part))
    q = sweep_call(last_kernel, "last_update", [f, matrix, bias, q] + halo, q, state)
    return (q.transpose(2, 0, 1, 3), mean)


def solution(mesh):
    placed = P(None, "gx", "gy", "gz")
    return jax.shard_map(
        local,
        mesh=mesh,
        in_specs=(placed, placed),
        out_specs=(placed, P()),
        check_vma=False,
    )
```

time: 1140 us -> 243 us (0.21); the launches traced: 1120 us -> 242 us
  waiting for transfers between devices: 346 us -> 6.88 us
  other arithmetic: 233 us -> 0 us
  matrix products: 182 us -> 0 us
  Pallas kernels: 0 us -> 171 us
  blocking collectives: 171 us -> 0 us
  local copies, waits for them, and re-layouts: 127 us -> 14.5 us
  between operations: 15 us -> 1.04 us
    psum x2 -> x0, waiting for transfers between devices: 332 us -> none  [fit(): lax.psum((counts, first_moment, scatter), ('gx', 'gy', 'gz'))]
    dot_general x68 -> x0, matrix products: 180 us -> none  [the longest x32 93.1 us: second(): lax.dot_general(weighted, flat_vox, contract, preferred_element_type=jnp....]
    another operation x11 -> x0, other arithmetic: 173 us -> none  [the longest x7 94.1 us: finish(): factor = jnp.linalg.cholesky(spread)]
    psum x2 -> x0, blocking collectives: 171 us -> none  [fit(): lax.psum((counts, first_moment, scatter), ('gx', 'gy', 'gz'))]
    pallas_call x0 -> x8, Pallas kernels: none -> 171 us  [the longest x2 72.9 us: summed(): pl.pallas_call(functools.partial(sum_kernel, sizes), name='sum_over_devic...]
    dynamic_slice x64 -> x0, local copies, waits for them, and re-layouts: 33.4 us -> none  [the longest x32 20.2 us: loglik(): scores = lax.map(per_class, (rounded, offset, biases))]
    dynamic_update_slice x32 -> x0, local copies, waits for them, and re-layouts: 30.3 us -> none  [loglik(): scores = lax.map(per_class, (rounded, offset, biases))]
    sub x34 -> x0, other arithmetic: 21.8 us -> none  [the longest x32 19.9 us: per_class(): return level - 0.5 * jnp.sum(whitened * whitened, axis=0)]
  transfers between devices with their start and end apart: 20 -> 18, of which waited for: 8 -> 4; matrix products, arithmetic and copies ran while one was open for 38% -> 2% of each run, Pallas kernels for 0% -> 44%
where the time goes in v1:
time: 243 us; the launch traced here: 242 us
  Pallas kernels  171 us (70%)
  starting transfers between devices  48.9 us (20%)
  local copies, waits for them, and re-layouts  14.5 us (6%)
  waiting for transfers between devices  6.88 us (3%)
    pallas_call x2, Pallas kernels, summed(): pl.pallas_call(functools.partial(sum_kernel, sizes), name='sum_over_devic...  72.9 us
    pallas_call x3, Pallas kernels, sweep_call(): pl.pallas_call(kernel, name=name, out_shape=out_shape, in_specs=[VMEM] *...  65.2 us
    ppermute x9, starting transfers between devices, halo_of(): got.append(lax.ppermute(last, axis, up))  28.8 us
    ppermute x9, starting transfers between devices, halo_of(): got.append(lax.ppermute(first, axis, down))  20.1 us
    pallas_call x1, Pallas kernels, moments(): pl.pallas_call(moments_kernel, name='moments', out_shape=(jax.ShapeDtypeS...  16.6 us
    pallas_call x2, Pallas kernels, finish(): pl.pallas_call(finish_kernel, name='finish', out_shape=(jax.ShapeDtypeStr...  16.2 us
    unnamed x43, local copies, waits for them, and re-layouts  9.25 us
  transfers between devices with their start and end apart: 18, of which 4 were waited for; matrix products, arithmetic and copies ran while one was open for 2% of the time, Pallas kernels for 44%

profile of v1, /device:TPU:1, one launch (start us, length us, event | category | flops | bytes accessed | tf_op | source)
XLA Modules:
  0.0 242.1 jit_solution(16718506442750811943)
XLA Ops:
  0.6 2.1 copy.21
  4.0 4.6 %collective-permute-start = (bf16[32,16,128]{2,1,0:T(8,128)(2,1)S(1)}, bf16[32,16,128]{2,1,0:T(8,128)(2,1)S(1)}, u32[]{:S(2)}, u32[]{:S(2)}) collective-permute-start(bf16[32,16,128]{2,1,0:T(8,128)(2,1)S(1)} %get-tuple-element.47), channel_id=1, source_target_pairs={{0,64},{64,128},{128,192},{1,65},{65,129},{129,193},{2,66},{66,130... | collective-permute-start | bytes 393224 | tf_op jit(solution)/shard_map/ppermute | solution.py:364
  8.6 5.1 %collective-permute-start.3 = (bf16[8,16,128]{2,1,0:T(8,128)(2,1)S(1)}, bf16[8,16,128]{2,1,0:T(8,128)(2,1)S(1)}, u32[]{:S(2)}, u32[]{:S(2)}) collective-permute-start(bf16[8,16,128]{2,1,0:T(8,128)(2,1)S(1)} %get-tuple-element.44), channel_id=1, source_target_pairs={{8,0},{16,8},{24,16},{32,24},{40,32},{48,40},{56,48},{9,1},{17,9},... | collective-permute-start | bytes 98312 | tf_op jit(solution)/shard_map/ppermute | solution.py:365
  13.8 1.9 collective-permute-start.2
  17.4 2.7 %copy.20 = bf16[32,8,32,128]{3,0,2,1:T(8,128)(2,1)} copy(bf16[32,8,32,128]{3,2,1,0:T(8,128)(2,1)S(1)} %copy-done.1) | data formatting | bytes 4194304 | tf_op args[0]
  20.0 16.6 %moments.1 = (f32[8,24,128]{2,1,0:T(8,128)}, bf16[1,4096]{1,0:T(2,128)(2,1)}, bf16[1,4096]{1,0:T(2,128)(2,1)}) custom-call(bf16[8,32,32,128]{3,2,1,0:T(8,128)(2,1)} %bitcast.32, bf16[8,32,16,128]{3,2,1,0:T(8,128)(2,1)} %copy.6.q_ref), custom_call_target="tpu_custom_call" | custom-call | tf_op jit(solution)/shard_map/moments/pallas_call | solution.py:91
  36.6 3.0 %collective-permute-start.4 = (bf16[1,4096]{1,0:T(2,128)(2,1)}, bf16[1,4096]{1,0:T(2,128)(2,1)S(1)}, u32[]{:S(2)}, u32[]{:S(2)}) collective-permute-start(bf16[1,4096]{1,0:T(2,128)(2,1)} %get-tuple-element.21), channel_id=1, source_target_pairs={{0,1},{1,2},{2,3},{3,4},{4,5},{5,6},{6,7},{8,9},{9,10},{10,11},{11... | collective-permute-start | bytes 24584 | tf_op jit(solution)/shard_map/ppermute | solution.py:364
  41.9 34.7 %sum_over_devices.2.sum_ref = f32[8,24,128]{2,1,0:T(8,128)} custom-call(f32[8,24,128]{2,1,0:T(8,128)} %get-tuple-element.18.part_ref), custom_call_target="tpu_custom_call" | custom-call | tf_op jit(solution)/shard_map/sum_over_devices/pallas_call | solution.py:162
  76.7 8.1 %finish.2 = (bf16[512,128]{1,0:T(8,128)(2,1)}, f32[16,128]{1,0:T(8,128)}, f32[16,32]{1,0:T(8,128)}) custom-call(f32[8,24,128]{2,1,0:T(8,128)} %sum_over_devices.2.sum_ref), custom_call_target="tpu_custom_call" | custom-call | tf_op jit(solution)/shard_map/finish/pallas_call | solution.py:220
  85.5 22.8 %first_sweep.1 = (bf16[8,32,16,128]{3,2,1,0:T(8,128)(2,1)}, f32[8,32,16,128]{3,2,1,0:T(8,128)}, bf16[1,4096]{1,0:T(2,128)(2,1)}, bf16[1,4096]{1,0:T(2,128)(2,1)}) custom-call(bf16[8,32,32,128]{3,2,1,0:T(8,128)(2,1)} %bitcast.33, bf16[512,128]{1,0:T(8,128)(2,1)} %get-tuple-element.19.m_ref, f32[16,128]{1,0:T(8,128)} %get-tuple-element.20.b_ref, ...), custom_call_target="tpu_custom_call" | custom-call | tf_op jit(solution)/shard_map/first_sweep/pallas_call | solution.py:347
  110.6 4.0 %collective-permute-start.6 = (bf16[32,16,128]{2,1,0:T(8,128)(2,1)S(1)}, bf16[32,16,128]{2,1,0:T(8,128)(2,1)S(1)}, u32[]{:S(2)}, u32[]{:S(2)}) collective-permute-start(bf16[32,16,128]{2,1,0:T(8,128)(2,1)S(1)} %get-tuple-element.43), channel_id=1, source_target_pairs={{0,64},{64,128},{128,192},{1,65},{65,129},{129,193},{2,66},{66,130... | collective-permute-start | bytes 393224 | tf_op jit(solution)/shard_map/ppermute | solution.py:364
  115.4 2.9 %collective-permute-start.9 = (bf16[8,16,128]{2,1,0:T(8,128)(2,1)S(1)}, bf16[8,16,128]{2,1,0:T(8,128)(2,1)S(1)}, u32[]{:S(2)}, u32[]{:S(2)}) collective-permute-start(bf16[8,16,128]{2,1,0:T(8,128)(2,1)S(1)} %get-tuple-element.40), channel_id=1, source_target_pairs={{8,0},{16,8},{24,16},{32,24},{40,32},{48,40},{56,48},{9,1},{17,9},... | collective-permute-start | bytes 98312 | tf_op jit(solution)/shard_map/ppermute | solution.py:365
  118.3 2.7 %collective-permute-start.8 = (bf16[8,16,128]{2,1,0:T(8,128)(2,1)S(1)}, bf16[8,16,128]{2,1,0:T(8,128)(2,1)S(1)}, u32[]{:S(2)}, u32[]{:S(2)}) collective-permute-start(bf16[8,16,128]{2,1,0:T(8,128)(2,1)S(1)} %get-tuple-element.41), channel_id=1, source_target_pairs={{0,8},{8,16},{16,24},{24,32},{32,40},{40,48},{48,56},{1,9},{9,17},... | collective-permute-start | bytes 98312 | tf_op jit(solution)/shard_map/ppermute | solution.py:364
  121.0 2.6 %collective-permute-start.10 = (bf16[1,4096]{1,0:T(2,128)(2,1)}, bf16[1,4096]{1,0:T(2,128)(2,1)S(1)}, u32[]{:S(2)}, u32[]{:S(2)}) collective-permute-start(bf16[1,4096]{1,0:T(2,128)(2,1)} %get-tuple-element.25), channel_id=1, source_target_pairs={{0,1},{1,2},{2,3},{3,4},{4,5},{5,6},{6,7},{8,9},{9,10},{10,11},{11... | collective-permute-start | bytes 24584 | tf_op jit(solution)/shard_map/ppermute | solution.py:364
  126.0 3.7 %collective-permute-done.11.zhi = bf16[1,4096]{1,0:T(2,128)(2,1)S(1)} collective-permute-done((bf16[1,4096]{1,0:T(2,128)(2,1)}, bf16[1,4096]{1,0:T(2,128)(2,1)S(1)}, u32[]{:S(2)}, u32[]{:S(2)}) %collective-permute-start.11) | collective-permute-done | bytes 8224 | tf_op jit(solution)/shard_map/ppermute | solution.py:365
  130.4 24.2 %second_sweep.1 = (bf16[8,32,16,128]{3,2,1,0:T(8,128)(2,1)}, f32[8,24,128]{2,1,0:T(8,128)}, bf16[1,4096]{1,0:T(2,128)(2,1)}, bf16[1,4096]{1,0:T(2,128)(2,1)}) custom-call(bf16[8,32,32,128]{3,2,1,0:T(8,128)(2,1)} %bitcast.34, f32[8,32,16,128]{3,2,1,0:T(8,128)} %get-tuple-element.23.scores_ref, bf16[8,32,16,128]{3,2,1,0:T(8,128)(2,1)} %get-tuple-element.24.q_ref, ...), custom_call_target="tpu_custom_call" | custom-call | tf_op jit(solution)/shard_map/second_sweep/pallas_call | solution.py:347
  156.9 4.0 %collective-permute-start.12 = (bf16[32,16,128]{2,1,0:T(8,128)(2,1)S(1)}, bf16[32,16,128]{2,1,0:T(8,128)(2,1)S(1)}, u32[]{:S(2)}, u32[]{:S(2)}) collective-permute-start(bf16[32,16,128]{2,1,0:T(8,128)(2,1)S(1)} %get-tuple-element.39), channel_id=1, source_target_pairs={{0,64},{64,128},{128,192},{1,65},{65,129},{129,193},{2,66},{66,130... | collective-permute-start | bytes 393224 | tf_op jit(solution)/shard_map/ppermute | solution.py:364
  161.7 4.2 %collective-permute-start.15 = (bf16[8,16,128]{2,1,0:T(8,128)(2,1)S(1)}, bf16[8,16,128]{2,1,0:T(8,128)(2,1)S(1)}, u32[]{:S(2)}, u32[]{:S(2)}) collective-permute-start(bf16[8,16,128]{2,1,0:T(8,128)(2,1)S(1)} %get-tuple-element.36), channel_id=1, source_target_pairs={{8,0},{16,8},{24,16},{32,24},{40,32},{48,40},{56,48},{9,1},{17,9},... | collective-permute-start | bytes 98312 | tf_op jit(solution)/shard_map/ppermute | solution.py:365
  165.9 2.4 collective-permute-start.14
  168.3 3.6 %collective-permute-start.16 = (bf16[1,4096]{1,0:T(2,128)(2,1)}, bf16[1,4096]{1,0:T(2,128)(2,1)S(1)}, u32[]{:S(2)}, u32[]{:S(2)}) collective-permute-start(bf16[1,4096]{1,0:T(2,128)(2,1)} %get-tuple-element.31), channel_id=1, source_target_pairs={{0,1},{1,2},{2,3},{3,4},{4,5},{5,6},{6,7},{8,9},{9,10},{10,11},{11... | collective-permute-start | bytes 24584 | tf_op jit(solution)/shard_map/ppermute | solution.py:364
  174.4 38.2 %sum_over_devices.3.sum_ref = f32[8,24,128]{2,1,0:T(8,128)} custom-call(f32[8,24,128]{2,1,0:T(8,128)} %get-tuple-element.27.part_ref), custom_call_target="tpu_custom_call" | custom-call | tf_op jit(solution)/shard_map/sum_over_devices/pallas_call | solution.py:162
  212.6 8.1 %finish.3 = (bf16[512,128]{1,0:T(8,128)(2,1)}, f32[16,128]{1,0:T(8,128)}, f32[16,32]{1,0:T(8,128)}) custom-call(f32[8,24,128]{2,1,0:T(8,128)} %sum_over_devices.3.sum_ref), custom_call_target="tpu_custom_call" | custom-call | tf_op jit(solution)/shard_map/finish/pallas_call | solution.py:220
  221.4 18.2 %last_update.1 = bf16[8,32,16,128]{3,2,1,0:T(8,128)(2,1)} custom-call(bf16[8,32,32,128]{3,2,1,0:T(8,128)(2,1)} %bitcast.35, bf16[512,128]{1,0:T(8,128)(2,1)} %get-tuple-element.28.m_ref, f32[16,128]{1,0:T(8,128)} %get-tuple-element.29.b_ref, bf16[8,32,16,128]{3,2,1,0:T(8,128)(2,1)} %get-tuple-element.30.q_ref, bf16[32,16,128]{2,1,0:T(8,128)(2,1)} %copy-done.6, ...), custom_call_target="tpu_custom_call" | custom-call | tf_op jit(solution)/shard_map/last_update/pallas_call | solution.py:347
  239.6 2.5 %copy.12 = bf16[16,8,32,128]{3,2,1,0:T(8,128)(2,1)} copy(bf16[16,8,32,128]{3,0,2,1:T(8,128)(2,1)} %bitcast.37) | data formatting | bytes 2097152
  (70 shorter events, 18.4 us)
Async XLA Ops:
  0.6 15.1 %copy-start = (bf16[16,8,32,128]{3,2,1,0:T(8,128)(2,1)S(1)}, bf16[16,8,32,128]{3,2,1,0:T(8,128)(2,1)}, u32[]{:S(2)}) copy-start(bf16[16,8,32,128]{3,2,1,0:T(8,128)(2,1)} %param.3) | copy-start | bytes 3145732
  0.6 16.7 %copy-start.1 = (bf16[32,8,32,128]{3,2,1,0:T(8,128)(2,1)S(1)}, bf16[32,8,32,128]{3,2,1,0:T(8,128)(2,1)}, u32[]{:S(2)}) copy-start(bf16[32,8,32,128]{3,2,1,0:T(8,128)(2,1)} %param.2) | copy-start | bytes 6291460
  2.7 82.1 %collective-permute-start.1 = (bf16[32,16,128]{2,1,0:T(8,128)(2,1)S(1)}, bf16[32,16,128]{2,1,0:T(8,128)(2,1)S(1)}, u32[]{:S(2)}, u32[]{:S(2)}) collective-permute-start(bf16[32,16,128]{2,1,0:T(8,128)(2,1)S(1)} %get-tuple-element.46), channel_id=1, source_target_pairs={{64,0},{128,64},{192,128},{65,1},{129,65},{193,129},{66,2},{130,66... | collective-permute-start | bytes 393224 | tf_op jit(solution)/shard_map/ppermute | solution.py:365
  4.0 80.8 %collective-permute-start = (bf16[32,16,128]{2,1,0:T(8,128)(2,1)S(1)}, bf16[32,16,128]{2,1,0:T(8,128)(2,1)S(1)}, u32[]{:S(2)}, u32[]{:S(2)}) collective-permute-start(bf16[32,16,128]{2,1,0:T(8,128)(2,1)S(1)} %get-tuple-element.47), channel_id=1, source_target_pairs={{0,64},{64,128},{128,192},{1,65},{65,129},{129,193},{2,66},{66,130... | collective-permute-start | bytes 393224 | tf_op jit(solution)/shard_map/ppermute | solution.py:364
  8.6 76.1 %collective-permute-start.3 = (bf16[8,16,128]{2,1,0:T(8,128)(2,1)S(1)}, bf16[8,16,128]{2,1,0:T(8,128)(2,1)S(1)}, u32[]{:S(2)}, u32[]{:S(2)}) collective-permute-start(bf16[8,16,128]{2,1,0:T(8,128)(2,1)S(1)} %get-tuple-element.44), channel_id=1, source_target_pairs={{8,0},{16,8},{24,16},{32,24},{40,32},{48,40},{56,48},{9,1},{17,9},... | collective-permute-start | bytes 98312 | tf_op jit(solution)/shard_map/ppermute | solution.py:365
  13.8 71.0 %collective-permute-start.2 = (bf16[8,16,128]{2,1,0:T(8,128)(2,1)S(1)}, bf16[8,16,128]{2,1,0:T(8,128)(2,1)S(1)}, u32[]{:S(2)}, u32[]{:S(2)}) collective-permute-start(bf16[8,16,128]{2,1,0:T(8,128)(2,1)S(1)} %get-tuple-element.45), channel_id=1, source_target_pairs={{0,8},{8,16},{16,24},{24,32},{32,40},{40,48},{48,56},{1,9},{9,17},... | collective-permute-start | bytes 98312 | tf_op jit(solution)/shard_map/ppermute | solution.py:364
  36.6 4.0 %collective-permute-start.4 = (bf16[1,4096]{1,0:T(2,128)(2,1)}, bf16[1,4096]{1,0:T(2,128)(2,1)S(1)}, u32[]{:S(2)}, u32[]{:S(2)}) collective-permute-start(bf16[1,4096]{1,0:T(2,128)(2,1)} %get-tuple-element.21), channel_id=1, source_target_pairs={{0,1},{1,2},{2,3},{3,4},{4,5},{5,6},{6,7},{8,9},{9,10},{10,11},{11... | collective-permute-start | bytes 24584 | tf_op jit(solution)/shard_map/ppermute | solution.py:364
  40.6 44.2 %copy-start.14 = (bf16[1,4096]{1,0:T(2,128)(2,1)}, bf16[1,4096]{1,0:T(2,128)(2,1)S(1)}, u32[]{:S(2)}) copy-start(bf16[1,4096]{1,0:T(2,128)(2,1)S(1)} %collective-permute-done.4.zlo) | copy-start | bytes 24580
  40.6 44.1 %collective-permute-start.5 = (bf16[1,4096]{1,0:T(2,128)(2,1)}, bf16[1,4096]{1,0:T(2,128)(2,1)S(1)}, u32[]{:S(2)}, u32[]{:S(2)}) collective-permute-start(bf16[1,4096]{1,0:T(2,128)(2,1)} %get-tuple-element.22), channel_id=1, source_target_pairs={{1,0},{2,1},{3,2},{4,3},{5,4},{6,5},{7,6},{9,8},{10,9},{11,10},{12... | collective-permute-start | bytes 24584 | tf_op jit(solution)/shard_map/ppermute | solution.py:365
  84.8 0.7 copy-start.3
  109.3 20.3 %collective-permute-start.7 = (bf16[32,16,128]{2,1,0:T(8,128)(2,1)S(1)}, bf16[32,16,128]{2,1,0:T(8,128)(2,1)S(1)}, u32[]{:S(2)}, u32[]{:S(2)}) collective-permute-start(bf16[32,16,128]{2,1,0:T(8,128)(2,1)S(1)} %get-tuple-element.42), channel_id=1, source_target_pairs={{64,0},{128,64},{192,128},{65,1},{129,65},{193,129},{66,2},{130,66... | collective-permute-start | bytes 393224 | tf_op jit(solution)/shard_map/ppermute | solution.py:365
  110.6 19.1 %collective-permute-start.6 = (bf16[32,16,128]{2,1,0:T(8,128)(2,1)S(1)}, bf16[32,16,128]{2,1,0:T(8,128)(2,1)S(1)}, u32[]{:S(2)}, u32[]{:S(2)}) collective-permute-start(bf16[32,16,128]{2,1,0:T(8,128)(2,1)S(1)} %get-tuple-element.43), channel_id=1, source_target_pairs={{0,64},{64,128},{128,192},{1,65},{65,129},{129,193},{2,66},{66,130... | collective-permute-start | bytes 393224 | tf_op jit(solution)/shard_map/ppermute | solution.py:364
  115.4 14.2 %collective-permute-start.9 = (bf16[8,16,128]{2,1,0:T(8,128)(2,1)S(1)}, bf16[8,16,128]{2,1,0:T(8,128)(2,1)S(1)}, u32[]{:S(2)}, u32[]{:S(2)}) collective-permute-start(bf16[8,16,128]{2,1,0:T(8,128)(2,1)S(1)} %get-tuple-element.40), channel_id=1, source_target_pairs={{8,0},{16,8},{24,16},{32,24},{40,32},{48,40},{56,48},{9,1},{17,9},... | collective-permute-start | bytes 98312 | tf_op jit(solution)/shard_map/ppermute | solution.py:365
  118.3 11.4 %collective-permute-start.8 = (bf16[8,16,128]{2,1,0:T(8,128)(2,1)S(1)}, bf16[8,16,128]{2,1,0:T(8,128)(2,1)S(1)}, u32[]{:S(2)}, u32[]{:S(2)}) collective-permute-start(bf16[8,16,128]{2,1,0:T(8,128)(2,1)S(1)} %get-tuple-element.41), channel_id=1, source_target_pairs={{0,8},{8,16},{16,24},{24,32},{32,40},{40,48},{48,56},{1,9},{9,17},... | collective-permute-start | bytes 98312 | tf_op jit(solution)/shard_map/ppermute | solution.py:364
  121.0 3.7 %collective-permute-start.10 = (bf16[1,4096]{1,0:T(2,128)(2,1)}, bf16[1,4096]{1,0:T(2,128)(2,1)S(1)}, u32[]{:S(2)}, u32[]{:S(2)}) collective-permute-start(bf16[1,4096]{1,0:T(2,128)(2,1)} %get-tuple-element.25), channel_id=1, source_target_pairs={{0,1},{1,2},{2,3},{3,4},{4,5},{5,6},{6,7},{8,9},{9,10},{10,11},{11... | collective-permute-start | bytes 24584 | tf_op jit(solution)/shard_map/ppermute | solution.py:364
  124.7 5.0 %copy-start.17 = (bf16[1,4096]{1,0:T(2,128)(2,1)}, bf16[1,4096]{1,0:T(2,128)(2,1)S(1)}, u32[]{:S(2)}) copy-start(bf16[1,4096]{1,0:T(2,128)(2,1)S(1)} %collective-permute-done.10.zlo) | copy-start | bytes 24580
  124.7 4.9 %collective-permute-start.11 = (bf16[1,4096]{1,0:T(2,128)(2,1)}, bf16[1,4096]{1,0:T(2,128)(2,1)S(1)}, u32[]{:S(2)}, u32[]{:S(2)}) collective-permute-start(bf16[1,4096]{1,0:T(2,128)(2,1)} %get-tuple-element.26), channel_id=1, source_target_pairs={{1,0},{2,1},{3,2},{4,3},{5,4},{6,5},{7,6},{9,8},{10,9},{11,10},{12... | collective-permute-start | bytes 24584 | tf_op jit(solution)/shard_map/ppermute | solution.py:365
  155.6 65.1 %collective-permute-start.13 = (bf16[32,16,128]{2,1,0:T(8,128)(2,1)S(1)}, bf16[32,16,128]{2,1,0:T(8,128)(2,1)S(1)}, u32[]{:S(2)}, u32[]{:S(2)}) collective-permute-start(bf16[32,16,128]{2,1,0:T(8,128)(2,1)S(1)} %get-tuple-element.38), channel_id=1, source_target_pairs={{64,0},{128,64},{192,128},{65,1},{129,65},{193,129},{66,2},{130,66... | collective-permute-start | bytes 393224 | tf_op jit(solution)/shard_map/ppermute | solution.py:365
  156.9 63.9 %collective-permute-start.12 = (bf16[32,16,128]{2,1,0:T(8,128)(2,1)S(1)}, bf16[32,16,128]{2,1,0:T(8,128)(2,1)S(1)}, u32[]{:S(2)}, u32[]{:S(2)}) collective-permute-start(bf16[32,16,128]{2,1,0:T(8,128)(2,1)S(1)} %get-tuple-element.39), channel_id=1, source_target_pairs={{0,64},{64,128},{128,192},{1,65},{65,129},{129,193},{2,66},{66,130... | collective-permute-start | bytes 393224 | tf_op jit(solution)/shard_map/ppermute | solution.py:364
  161.7 59.0 %collective-permute-start.15 = (bf16[8,16,128]{2,1,0:T(8,128)(2,1)S(1)}, bf16[8,16,128]{2,1,0:T(8,128)(2,1)S(1)}, u32[]{:S(2)}, u32[]{:S(2)}) collective-permute-start(bf16[8,16,128]{2,1,0:T(8,128)(2,1)S(1)} %get-tuple-element.36), channel_id=1, source_target_pairs={{8,0},{16,8},{24,16},{32,24},{40,32},{48,40},{56,48},{9,1},{17,9},... | collective-permute-start | bytes 98312 | tf_op jit(solution)/shard_map/ppermute | solution.py:365
  165.9 54.8 %collective-permute-start.14 = (bf16[8,16,128]{2,1,0:T(8,128)(2,1)S(1)}, bf16[8,16,128]{2,1,0:T(8,128)(2,1)S(1)}, u32[]{:S(2)}, u32[]{:S(2)}) collective-permute-start(bf16[8,16,128]{2,1,0:T(8,128)(2,1)S(1)} %get-tuple-element.37), channel_id=1, source_target_pairs={{0,8},{8,16},{16,24},{24,32},{32,40},{40,48},{48,56},{1,9},{9,17},... | collective-permute-start | bytes 98312 | tf_op jit(solution)/shard_map/ppermute | solution.py:364
  168.3 4.7 %collective-permute-start.16 = (bf16[1,4096]{1,0:T(2,128)(2,1)}, bf16[1,4096]{1,0:T(2,128)(2,1)S(1)}, u32[]{:S(2)}, u32[]{:S(2)}) collective-permute-start(bf16[1,4096]{1,0:T(2,128)(2,1)} %get-tuple-element.31), channel_id=1, source_target_pairs={{0,1},{1,2},{2,3},{3,4},{4,5},{5,6},{6,7},{8,9},{9,10},{10,11},{11... | collective-permute-start | bytes 24584 | tf_op jit(solution)/shard_map/ppermute | solution.py:364
  173.0 47.8 %copy-start.15 = (bf16[1,4096]{1,0:T(2,128)(2,1)}, bf16[1,4096]{1,0:T(2,128)(2,1)S(1)}, u32[]{:S(2)}) copy-start(bf16[1,4096]{1,0:T(2,128)(2,1)S(1)} %collective-permute-done.16.zlo) | copy-start | bytes 24580
  173.0 47.7 %collective-permute-start.17 = (bf16[1,4096]{1,0:T(2,128)(2,1)}, bf16[1,4096]{1,0:T(2,128)(2,1)S(1)}, u32[]{:S(2)}, u32[]{:S(2)}) collective-permute-start(bf16[1,4096]{1,0:T(2,128)(2,1)} %get-tuple-element.32), channel_id=1, source_target_pairs={{1,0},{2,1},{3,2},{4,3},{5,4},{6,5},{7,6},{9,8},{10,9},{11,10},{12... | collective-permute-start | bytes 24584 | tf_op jit(solution)/shard_map/ppermute | solution.py:365
  (14 other events, 8.8 us)

commit v2 on v1

--- a/solution.py
+++ b/solution.py
@@ -12,8 +12,9 @@
 CLASSES = 16
 LANES = 128
 GROUP = 8
-PIECES = 8
-PIECE_ROWS = 24
+PIECES = 16
+PIECE_ROWS = 9
+HALVES = 2
 AUG = 48
 
 beta_coupling = 1.0
@@ -55,18 +56,18 @@
 
 
 def pack_moments(total, out_ref):
-    rows_per = FEATS // PIECES
-    for piece in range(PIECES):
+    rows_per = LANES // FEATS
+    for part in range(FEATS // rows_per):
         blocks = []
         for r in range(rows_per):
-            row = piece * rows_per + r
+            row = part * rows_per + r
             blocks.append(total[pl.ds(row, CLASSES, stride=FEATS), :][:, :FEATS])
-        out_ref[piece, :CLASSES, :] = jnp.concatenate(blocks, axis=1)
-        if piece < 2:
-            start = CLASSES * FEATS + 8 * piece
-            out_ref[piece, CLASSES:, :] = total[start : start + 8, :]
-        else:
-            out_ref[piece, CLASSES:, :] = jnp.zeros((8, LANES), jnp.float32)
+        block = jnp.concatenate(blocks, axis=1)
+        out_ref[2 * part, :8, :] = block[:8]
+        out_ref[2 * part + 1, :8, :] = block[8:]
+    for k in range(CLASSES):
+        start = CLASSES * FEATS + k
+        out_ref[k, 8:9, :] = total[start : start + 1, :]
 
 
 def moments_kernel(f_ref, q_ref, out_ref, low_ref, high_ref, total):
@@ -102,94 +103,187 @@
     )(f, q)
 
 
-def sum_kernel(sizes, part_ref, out_ref, held_y, held_z, held_x, full, send, recv):
-    me = {axis: lax.axis_index(axis) for axis in AXES}
-
-    def partner(axis, d):
-        return lax.rem(me[axis] + d, sizes[axis])
-
+def places(sizes):
+    gx, gy, gz = (lax.axis_index(axis) for axis in AXES)
+    depth = sizes["gz"] // HALVES
+    half, y = lax.div(gz, depth), lax.rem(gz, depth)
+    ring, plane = gy * HALVES + half, gx * depth + y
+    rings, planes = sizes["gy"] * HALVES, sizes["gx"] * depth
+
+    def in_ring(d):
+        there = lax.rem(ring + d, rings)
+        return there, {
+            "gy": lax.div(there, HALVES),
+            "gz": lax.rem(there, HALVES) * depth + y,
+        }
+
+    def in_plane(d):
+        there = lax.rem(plane + d, planes)
+        return there, {"gx": lax.div(there, depth), "gz": half * depth + lax.rem(there, depth)}
+
+    return (ring, rings, in_ring), (plane, planes, in_plane)
+
+
+def beside(sizes, axis, d):
+    return {axis: lax.rem(lax.axis_index(axis) + d + sizes[axis], sizes[axis])}
+
+
+def meet(devices):
     barrier = pltpu.get_barrier_semaphore()
-    for axis in AXES:
-        for d in range(1, sizes[axis]):
-            pl.semaphore_signal(
-                barrier, inc=1, device_id={axis: partner(axis, d)}, device_id_type=MESH
-            )
-    pl.semaphore_wait(barrier, sum(sizes[axis] - 1 for axis in AXES))
-
-    def exchange(stage, axis, source, held):
-        copies = []
-        for d in range(1, sizes[axis]):
-            there = partner(axis, d)
-            copies.append(
-                pltpu.make_async_remote_copy(
-                    src_ref=source(there),
-                    dst_ref=held.at[me[axis]],
-                    send_sem=send.at[stage, d],
-                    recv_sem=recv.at[stage, d],
-                    device_id={axis: there},
-                    device_id_type=MESH,
-                )
-            )
-        for copy in copies:
-            copy.start()
-        for copy in copies:
-            copy.wait()
-
-    def added(held, count):
-        value = held[0]
+    for device in devices:
+        pl.semaphore_signal(barrier, inc=1, device_id=device, device_id_type=MESH)
+    pl.semaphore_wait(barrier, len(devices))
+
+
+def remote(source, target, send, recv, device):
+    copy = pltpu.make_async_remote_copy(
+        src_ref=source, dst_ref=target, send_sem=send, recv_sem=recv,
+        device_id=device, device_id_type=MESH,
+    )
+    copy.start()
+    return copy
+
+
+def start_halo(sizes, q_ref, low_ref, high_ref, halo, send, recv):
+    last_x, last_y = q_ref.shape[0] - 1, q_ref.shape[1] - 1
+    faces = {
+        "gx": (q_ref.at[0], q_ref.at[last_x]),
+        "gy": (q_ref.at[:, 0], q_ref.at[:, last_y]),
+        "gz": (low_ref, high_ref),
+    }
+    copies = []
+    for n, (axis, (first, last)) in enumerate(faces.items()):
+        up, down = 2 * n, 2 * n + 1
+        copies.append(
+            remote(last, halo[up], send.at[up], recv.at[up], beside(sizes, axis, 1))
+        )
+        copies.append(
+            remote(first, halo[down], send.at[down], recv.at[down], beside(sizes, axis, -1))
+        )
+    return copies
+
+
+def end_halo(sizes, copies, halo):
+    for copy in copies:
+        copy.wait()
+    for n, axis in enumerate(AXES):
+        for ref, edge in ((halo[2 * n], 0), (halo[2 * n + 1], sizes[axis] - 1)):
+
+            @pl.when(lax.axis_index(axis) == edge)
+            def _(ref=ref):
+                ref[...] = jnp.zeros_like(ref)
+
+
+def halo_kernel(sizes, q_ref, low_ref, high_ref, *rest):
+    halo, (send, recv) = rest[:6], rest[6:]
+    meet([beside(sizes, axis, d) for axis in AXES for d in (1, -1)])
+    end_halo(sizes, start_halo(sizes, q_ref, low_ref, high_ref, halo, send, recv), halo)
+
+
+def sum_kernel(sizes, part_ref, q_ref, low_ref, high_ref, out_ref, *rest):
+    halo, (held, planar, full, send, recv, halo_send, halo_recv) = rest[:6], rest[6:]
+    (ring, rings, in_ring), (plane, planes, in_plane) = places(sizes)
+    devices = [in_ring(d)[1] for d in range(1, rings)]
+    devices += [in_plane(d)[1] for d in range(1, planes)]
+    meet(devices + [beside(sizes, "gz", 1), beside(sizes, "gz", -1)])
+    group = PIECES // rings
+
+    def added(ref, count):
+        value = ref[0]
         for i in range(1, count):
-            value = value + held[i]
+            value = value + ref[i]
         return value
 
-    y, z, x = me["gy"], me["gz"], me["gx"]
-    group = PIECES // sizes["gy"]
-    held_y[y] = part_ref[pl.ds(y * group, group)]
-    exchange(0, "gy", lambda there: part_ref.at[pl.ds(there * group, group)], held_y)
-    held_z[z] = added(held_y, sizes["gy"])
-    exchange(1, "gz", lambda there: held_z.at[z], held_z)
-    held_x[x] = added(held_z, sizes["gz"])
-    exchange(2, "gx", lambda there: held_x.at[x], held_x)
-    full[y] = added(held_x, sizes["gx"])
-    exchange(3, "gy", lambda there: full.at[y], full)
-    for i in range(sizes["gy"]):
-        out_ref[pl.ds(i * group, group)] = full[i]
-
-
-def summed(part):
+    held[ring] = part_ref[pl.ds(ring * group, group)]
+    copies = []
+    for d in range(1, rings):
+        there, device = in_ring(d)
+        source = part_ref.at[pl.ds(there * group, group)]
+        copies.append(remote(source, held.at[ring], send.at[0, d], recv.at[0, d], device))
+    halo_copies = start_halo(sizes, q_ref, low_ref, high_ref, halo, halo_send, halo_recv)
+    for copy in copies:
+        copy.wait()
+    planar[plane] = added(held, rings)
+    copies = []
+    for d in range(1, planes):
+        _, device = in_plane(d)
+        place = planar.at[plane]
+        copies.append(remote(place, place, send.at[1, d], recv.at[1, d], device))
+    for copy in copies:
+        copy.wait()
+    full[ring] = added(planar, planes)
+    copies = []
+    for d in range(1, rings):
+        _, device = in_ring(d)
+        place = full.at[ring]
+        copies.append(remote(place, place, send.at[2, d], recv.at[2, d], device))
+    for copy in copies:
+        copy.wait()
+    for i in range(rings):
+        out_ref[i * group : (i + 1) * group] = full[i]
+    end_halo(sizes, halo_copies, halo)
+
+
+def halo_shapes(q, low):
+    plane_x = jax.ShapeDtypeStruct(q.shape[1:], q.dtype)
+    plane_y = jax.ShapeDtypeStruct((q.shape[0],) + q.shape[2:], q.dtype)
+    plane_z = jax.ShapeDtypeStruct(low.shape, low.dtype)
+    return (plane_x, plane_x, plane_y, plane_y, plane_z, plane_z)
+
+
+def halo_of(q, low, high):
     sizes = {axis: lax.axis_size(axis) for axis in AXES}
-    most = max(sizes.values())
-    block = (PIECES // sizes["gy"], PIECE_ROWS, LANES)
     return pl.pallas_call(
+        functools.partial(halo_kernel, sizes),
+        name="halo",
+        out_shape=halo_shapes(q, low),
+        in_specs=[VMEM] * 3,
+        out_specs=(VMEM,) * 6,
+        scratch_shapes=[pltpu.SemaphoreType.DMA((6,)), pltpu.SemaphoreType.DMA((6,))],
+        compiler_params=pltpu.CompilerParams(collective_id=1, has_side_effects=True),
+    )(q, low, high)
+
+
+def summed(part, q, low, high):
+    sizes = {axis: lax.axis_size(axis) for axis in AXES}
+    rings, planes = sizes["gy"] * HALVES, sizes["gx"] * (sizes["gz"] // HALVES)
+    block = (PIECES // rings, PIECE_ROWS, LANES)
+    most = max(rings, planes)
+    total, *halo = pl.pallas_call(
         functools.partial(sum_kernel, sizes),
-        name="sum_over_devices",
-        out_shape=jax.ShapeDtypeStruct(part.shape, jnp.float32),
-        in_specs=[VMEM],
-        out_specs=VMEM,
+        name="sum_and_halo",
+        out_shape=(jax.ShapeDtypeStruct(part.shape, jnp.float32),) + halo_shapes(q, low),
+        in_specs=[VMEM] * 4,
+        out_specs=(VMEM,) * 7,
         scratch_shapes=[
-            pltpu.VMEM((sizes["gy"],) + block, jnp.float32),
-            pltpu.VMEM((sizes["gz"],) + block, jnp.float32),
-            pltpu.VMEM((sizes["gx"],) + block, jnp.float32),
-            pltpu.VMEM((sizes["gy"],) + block, jnp.float32),
-            pltpu.SemaphoreType.DMA((4, most)),
-            pltpu.SemaphoreType.DMA((4, most)),
+            pltpu.VMEM((rings,) + block, jnp.float32),
+            pltpu.VMEM((planes,) + block, jnp.float32),
+            pltpu.VMEM((rings,) + block, jnp.float32),
+            pltpu.SemaphoreType.DMA((3, most)),
+            pltpu.SemaphoreType.DMA((3, most)),
+            pltpu.SemaphoreType.DMA((6,)),
+            pltpu.SemaphoreType.DMA((6,)),
         ],
         compiler_params=pltpu.CompilerParams(collective_id=0, has_side_effects=True),
-    )(part)
+    )(part, q, low, high)
+    return total, halo
 
 
 def finish_kernel(sum_ref, matrix_ref, bias_ref, mean_ref):
-    last = jnp.concatenate([sum_ref[0, CLASSES:, :], sum_ref[1, CLASSES:, :]], axis=0)
+    last = jnp.concatenate([sum_ref[k, 8:9, :] for k in range(CLASSES)], axis=0)
     counts = last[:, FEATS : FEATS + 1]
     mean = last[:, :FEATS] / counts
     mean_ref[...] = mean
     total_weight = jnp.sum(counts, axis=0, keepdims=True)
     lane = lax.broadcasted_iota(jnp.int32, (CLASSES, LANES), 1)
     small = lax.broadcasted_iota(jnp.int32, (CLASSES, FEATS), 1)
-    rows_per = FEATS // PIECES
+    rows_per = LANES // FEATS
     rows = []
     for i in range(FEATS):
         start = (i % rows_per) * FEATS
-        second = sum_ref[i // rows_per, :CLASSES, start : start + FEATS]
+        part = 2 * (i // rows_per)
+        second = jnp.concatenate([sum_ref[part, :8, :], sum_ref[part + 1, :8, :]], axis=0)
+        second = second[:, start : start + FEATS]
         spread = second / counts - mean[:, i : i + 1] * mean + jnp.where(small == i, ridge, 0.0)
         unit = jnp.where(small == i, 1.0, 0.0)
         shift = jnp.where(small == 0, mean[:, i : i + 1], 0.0)
@@ -250,8 +344,8 @@
     total = total + block(0, 1).astype(jnp.float32) + block(0, -1).astype(jnp.float32)
     a = lax.broadcasted_iota(jnp.int32, (LANES, LANES), 0)
     b = lax.broadcasted_iota(jnp.int32, (LANES, LANES), 1)
-    beside = jnp.where((a == b + 1) | (a + 1 == b), 1.0, 0.0).astype(jnp.bfloat16)
-    total = total + jnp.dot(block(0, 0), beside, preferred_element_type=jnp.float32)
+    shift = jnp.where((a == b + 1) | (a + 1 == b), 1.0, 0.0).astype(jnp.bfloat16)
+    total = total + jnp.dot(block(0, 0), shift, preferred_element_type=jnp.float32)
     width = GROUP * CLASSES
     where = pl.ds(pl.multiple_of(c * width, width), width)
     side = lax.broadcasted_iota(jnp.int32, (8, width), 0)
@@ -354,18 +448,6 @@
     )(*operands)
 
 
-def halo_of(q, low, high):
-    faces = {"gx": (q[0], q[-1]), "gy": (q[:, 0], q[:, -1]), "gz": (low, high)}
-    got = []
-    for axis, (first, last) in faces.items():
-        count = lax.axis_size(axis)
-        up = [(i, i + 1) for i in range(count - 1)]
-        down = [(j, i) for i, j in up]
-        got.append(lax.ppermute(last, axis, up))
-        got.append(lax.ppermute(first, axis, down))
-    return got
-
-
 def local(features, posteriors):
     f = features.transpose(1, 2, 0, 3)
     q = posteriors.transpose(1, 2, 0, 3)
@@ -376,18 +458,18 @@
     total = pltpu.VMEM((CLASSES * FEATS + CLASSES, LANES), jnp.float32)
 
     part, low, high = moments(f, q)
-    halo = halo_of(q, low, high)
-    matrix, bias, _ = finish(summed(part))
+    total_sum, halo = summed(part, q, low, high)
+    matrix, bias, _ = finish(total_sum)
     q, scores, low, high = sweep_call(
-        first_kernel, "first_sweep", [f, matrix, bias, q] + halo, q,
+        first_kernel, "first_sweep", [f, matrix, bias, q, *halo], q,
         (state, scores_shape, face, face))
     halo = halo_of(q, low, high)
     q, part, low, high = sweep_call(
-        second_kernel, "second_sweep", [f, scores, q] + halo, q,
+        second_kernel, "second_sweep", [f, scores, q, *halo], q,
         (state, sums, face, face), [total])
-    halo = halo_of(q, low, high)
-    matrix, bias, mean = finish(summed(part))
-    q = sweep_call(last_kernel, "last_update", [f, matrix, bias, q] + halo, q, state)
+    total_sum, halo = summed(part, q, low, high)
+    matrix, bias, mean = finish(total_sum)
+    q = sweep_call(last_kernel, "last_update", [f, matrix, bias, q, *halo], q, state)
     return (q.transpose(2, 0, 1, 3), mean)
 
 

time: 243 us -> 170 us (0.70)
  starting transfers between devices: 48.9 us -> 0 us
  Pallas kernels: 171 us -> 161 us
  waiting for transfers between devices: 6.88 us -> 0 us
  local copies, waits for them, and re-layouts: 14.5 us -> 8.19 us
    ppermute x18 -> x0, starting transfers between devices: 48.9 us -> none  [the longest x9 28.8 us: halo_of(): got.append(lax.ppermute(last, axis, up))]
    pallas_call x2 -> x3, Pallas kernels: 72.9 us -> 63.1 us  [the longest x2 51.6 us: summed(): pl.pallas_call(functools.partial(sum_kernel, sizes), name='sum_and_halo',...]
    ppermute x18 -> x0, waiting for transfers between devices: 6.88 us -> none  [the longest x9 3.68 us: halo_of(): got.append(lax.ppermute(first, axis, down))]
    squeeze x6 -> x0, local copies, waits for them, and re-layouts: 3.57 us -> none  [halo_of(): faces = {'gx': (q[0], q[-1]), 'gy': (q[:, 0], q[:, -1]), 'gz': (low, high)}]
    unnamed x43 -> x5, local copies, waits for them, and re-layouts: 9.25 us -> 8.19 us
  transfers between devices with their start and end apart: 18 -> 0, of which waited for: 4 -> 0; matrix products, arithmetic and copies ran while one was open for 2% -> 0% of each run, Pallas kernels for 44% -> 0%
where the time goes in v2:
time: 170 us
  Pallas kernels  161 us (95%)
  local copies, waits for them, and re-layouts  8.19 us (5%)
    pallas_call x3, Pallas kernels, sweep_call(): pl.pallas_call(kernel, name=name, out_shape=out_shape, in_specs=[VMEM] *...  65.3 us
    pallas_call x2, Pallas kernels, summed(): pl.pallas_call(functools.partial(sum_kernel, sizes), name='sum_and_halo',...  51.6 us
    pallas_call x1, Pallas kernels, moments(): pl.pallas_call(moments_kernel, name='moments', out_shape=(jax.ShapeDtypeS...  16.5 us
    pallas_call x2, Pallas kernels, finish(): pl.pallas_call(finish_kernel, name='finish', out_shape=(jax.ShapeDtypeStr...  16.1 us
    pallas_call x1, Pallas kernels, halo_of(): pl.pallas_call(functools.partial(halo_kernel, sizes), name='halo', out_sh...  11.5 us
    unnamed x5, local copies, waits for them, and re-layouts  8.19 us

profile of v2, /device:TPU:1, one launch (start us, length us, event | category | flops | bytes accessed | tf_op | source)
XLA Modules:
  0.0 169.8 jit_solution(7536203898148769483)
XLA Ops:
  0.6 0.0 copy-start
  0.6 3.0 %copy.10 = bf16[16,8,32,128]{3,0,2,1:T(8,128)(2,1)} copy(bf16[16,8,32,128]{3,2,1,0:T(8,128)(2,1)} %param.3) | data formatting | bytes 2097152 | tf_op args[1]
  3.7 0.0 copy-done
  3.7 2.7 %copy.9 = bf16[32,8,32,128]{3,0,2,1:T(8,128)(2,1)} copy(bf16[32,8,32,128]{3,2,1,0:T(8,128)(2,1)S(1)} %copy-done) | data formatting | bytes 4194304 | tf_op args[0]
  6.4 16.5 %moments.1 = (f32[16,9,128]{2,1,0:T(8,128)}, bf16[1,4096]{1,0:T(2,128)(2,1)}, bf16[1,4096]{1,0:T(2,128)(2,1)}) custom-call(bf16[8,32,32,128]{3,2,1,0:T(8,128)(2,1)} %bitcast.7, bf16[8,32,16,128]{3,2,1,0:T(8,128)(2,1)} %bitcast.11), custom_call_target="tpu_custom_call" | custom-call | tf_op jit(solution)/shard_map/moments/pallas_call | solution.py:92
  22.8 28.3 %sum_and_halo.2 = (f32[16,9,128]{2,1,0:T(8,128)}, bf16[32,16,128]{2,1,0:T(8,128)(2,1)}, bf16[32,16,128]{2,1,0:T(8,128)(2,1)}, bf16[8,16,128]{2,1,0:T(8,128)(2,1)...) custom-call(f32[16,9,128]{2,1,0:T(8,128)} %get-tuple-element.38.part_ref, ...), custom_call_target="tpu_custom_call" | custom-call | tf_op jit(solution)/shard_map/sum_and_halo/pallas_call | solution.py:252
  51.2 8.0 %finish.2 = (bf16[512,128]{1,0:T(8,128)(2,1)}, f32[16,128]{1,0:T(8,128)}, f32[16,32]{1,0:T(8,128)}) custom-call(f32[16,9,128]{2,1,0:T(8,128)} %get-tuple-element.41.sum_ref), custom_call_target="tpu_custom_call" | custom-call | tf_op jit(solution)/shard_map/finish/pallas_call | solution.py:314
  59.2 22.8 %first_sweep.1 = (bf16[8,32,16,128]{3,2,1,0:T(8,128)(2,1)}, f32[8,32,16,128]{3,2,1,0:T(8,128)}, bf16[1,4096]{1,0:T(2,128)(2,1)}, bf16[1,4096]{1,0:T(2,128)(2,1)}) custom-call(bf16[8,32,32,128]{3,2,1,0:T(8,128)(2,1)} %bitcast.8, bf16[512,128]{1,0:T(8,128)(2,1)} %get-tuple-element.42.m_ref, f32[16,128]{1,0:T(8,128)} %get-tuple-element.43.b_ref, ...), custom_call_target="tpu_custom_call" | custom-call | tf_op jit(solution)/shard_map/first_sweep/pallas_call | solution.py:441
  82.0 11.5 %halo.1 = (bf16[32,16,128]{2,1,0:T(8,128)(2,1)}, bf16[32,16,128]{2,1,0:T(8,128)(2,1)}, bf16[8,16,128]{2,1,0:T(8,128)(2,1)}, bf16[8,16,128]{2,1,0:T(8,128)(2,1)},...) custom-call(bf16[8,32,16,128]{3,2,1,0:T(8,128)(2,1)} %get-tuple-element.51.q_ref, ...), custom_call_target="tpu_custom_call" | custom-call | tf_op jit(solution)/shard_map/halo/pallas_call | solution.py:236
  93.5 24.3 %second_sweep.1 = (bf16[8,32,16,128]{3,2,1,0:T(8,128)(2,1)}, f32[16,9,128]{2,1,0:T(8,128)}, bf16[1,4096]{1,0:T(2,128)(2,1)}, bf16[1,4096]{1,0:T(2,128)(2,1)}) custom-call(bf16[8,32,32,128]{3,2,1,0:T(8,128)(2,1)} %bitcast.9, f32[8,32,16,128]{3,2,1,0:T(8,128)} %get-tuple-element.50.scores_ref, bf16[8,32,16,128]{3,2,1,0:T(8,128)(2,1)} %get-tuple-element.51.q_ref, ...), custom_call_target="tpu_custom_call" | custom-call | tf_op jit(solution)/shard_map/second_sweep/pallas_call | solution.py:441
  117.7 23.3 %sum_and_halo.3 = (f32[16,9,128]{2,1,0:T(8,128)}, bf16[32,16,128]{2,1,0:T(8,128)(2,1)}, bf16[32,16,128]{2,1,0:T(8,128)(2,1)}, bf16[8,16,128]{2,1,0:T(8,128)(2,1)...) custom-call(f32[16,9,128]{2,1,0:T(8,128)} %get-tuple-element.60.part_ref, ...), custom_call_target="tpu_custom_call" | custom-call | tf_op jit(solution)/shard_map/sum_and_halo/pallas_call | solution.py:252
  141.0 8.0 %finish.3 = (bf16[512,128]{1,0:T(8,128)(2,1)}, f32[16,128]{1,0:T(8,128)}, f32[16,32]{1,0:T(8,128)}) custom-call(f32[16,9,128]{2,1,0:T(8,128)} %get-tuple-element.64.sum_ref), custom_call_target="tpu_custom_call" | custom-call | tf_op jit(solution)/shard_map/finish/pallas_call | solution.py:314
  149.1 18.2 %last_update.1 = bf16[8,32,16,128]{3,2,1,0:T(8,128)(2,1)} custom-call(bf16[8,32,32,128]{3,2,1,0:T(8,128)(2,1)} %bitcast.10, bf16[512,128]{1,0:T(8,128)(2,1)} %get-tuple-element.65.m_ref, f32[16,128]{1,0:T(8,128)} %get-tuple-element.66.b_ref, bf16[8,32,16,128]{3,2,1,0:T(8,128)(2,1)} %get-tuple-element.61.q_ref, bf16[32,16,128]{2,1,0:T(8,128)(2,1)} %get-tuple-element.67.xlo, ...), custom_call_target="tpu_custom_call" | custom-call | tf_op jit(solution)/shard_map/last_update/pallas_call | solution.py:441
  167.3 2.5 %copy.6 = bf16[16,8,32,128]{3,2,1,0:T(8,128)(2,1)} copy(bf16[16,8,32,128]{3,0,2,1:T(8,128)(2,1)} %bitcast.14) | data formatting | bytes 2097152
Async XLA Ops:
  0.6 3.0 %copy-start = (bf16[32,8,32,128]{3,2,1,0:T(8,128)(2,1)S(1)}, bf16[32,8,32,128]{3,2,1,0:T(8,128)(2,1)}, u32[]{:S(2)}) copy-start(bf16[32,8,32,128]{3,2,1,0:T(8,128)(2,1)} %param.2) | copy-start | bytes 6291460

commit v3 on v2

--- a/solution.py
+++ b/solution.py
@@ -16,6 +16,10 @@
 PIECE_ROWS = 9
 HALVES = 2
 AUG = 48
+
+UNROLL = 8
+LIMIT = 20 << 20
+MATRIX_ROWS = 128
 
 beta_coupling = 1.0
 ridge = 0.1
@@ -83,7 +87,7 @@
         face_of(jnp.concatenate(posts, axis=0), low_ref, high_ref, c)
         return carry
 
-    lax.fori_loop(0, count_x * per_x, step, 0)
+    lax.fori_loop(0, count_x * per_x, step, 0, unroll=UNROLL)
     pack_moments(total, out_ref)
 
 
@@ -99,6 +103,7 @@
         ),
         in_specs=[VMEM] * 2,
         out_specs=(VMEM,) * 3,
+        compiler_params=pltpu.CompilerParams(vmem_limit_bytes=LIMIT),
         scratch_shapes=[pltpu.VMEM((CLASSES * FEATS + CLASSES, LANES), jnp.float32)],
     )(f, q)
 
@@ -240,7 +245,7 @@
         in_specs=[VMEM] * 3,
         out_specs=(VMEM,) * 6,
         scratch_shapes=[pltpu.SemaphoreType.DMA((6,)), pltpu.SemaphoreType.DMA((6,))],
-        compiler_params=pltpu.CompilerParams(collective_id=1, has_side_effects=True),
+        compiler_params=pltpu.CompilerParams(collective_id=1, vmem_limit_bytes=LIMIT, has_side_effects=True),
     )(q, low, high)
 
 
@@ -264,7 +269,7 @@
             pltpu.SemaphoreType.DMA((6,)),
             pltpu.SemaphoreType.DMA((6,)),
         ],
-        compiler_params=pltpu.CompilerParams(collective_id=0, has_side_effects=True),
+        compiler_params=pltpu.CompilerParams(collective_id=0, vmem_limit_bytes=LIMIT, has_side_effects=True),
     )(part, q, low, high)
     return total, halo
 
@@ -321,6 +326,7 @@
         ),
         in_specs=[VMEM],
         out_specs=(VMEM,) * 3,
+        compiler_params=pltpu.CompilerParams(vmem_limit_bytes=LIMIT),
     )(total)
 
 
@@ -371,11 +377,12 @@
         pair = jnp.concatenate([f_ref[x, y + g], f_ref[x, y + g + 1]], axis=1)
         pair = augmented(pair)
         total = None
-        for m in range(0, FEATS * CLASSES, 128):
+        for m in range(0, FEATS * CLASSES, MATRIX_ROWS):
             white = jnp.dot(
-                matrix_ref[m : m + 128, :AUG], pair, preferred_element_type=jnp.float32
+                matrix_ref[m : m + MATRIX_ROWS, :AUG], pair, preferred_element_type=jnp.float32
             )
-            square = jnp.sum((white * white).reshape(128 // CLASSES, CLASSES, 2 * LANES), axis=0)
+            white = (white * white).reshape(MATRIX_ROWS // CLASSES, CLASSES, 2 * LANES)
+            square = jnp.sum(white, axis=0)
             total = square if total is None else total + square
         parts.append(bias - 0.5 * total[:, :LANES])
         parts.append(bias - 0.5 * total[:, LANES:])
@@ -397,7 +404,7 @@
         face_of(q.reshape(GROUP * CLASSES, LANES), low_ref, high_ref, c)
         return carry
 
-    lax.fori_loop(0, count_x * per_x, step, 0)
+    lax.fori_loop(0, count_x * per_x, step, 0, unroll=UNROLL)
 
 
 def second_kernel(f_ref, scores_ref, q_ref, xlo, xhi, ylo, yhi, zlo, zhi,
@@ -417,7 +424,7 @@
         face_of(q.reshape(GROUP * CLASSES, LANES), low_ref, high_ref, c)
         return carry
 
-    lax.fori_loop(0, count_x * per_x, step, 0)
+    lax.fori_loop(0, count_x * per_x, step, 0, unroll=UNROLL)
     pack_moments(total, sum_ref)
 
 
@@ -432,7 +439,7 @@
         out_ref[x, pl.ds(y, GROUP)] = update(scores, near_of(padded, zlo, zhi, x, y, c))
         return carry
 
-    lax.fori_loop(0, count_x * per_x, step, 0)
+    lax.fori_loop(0, count_x * per_x, step, 0, unroll=UNROLL)
 
 
 def sweep_call(kernel, name, operands, q, out_shape, scratch=()):
@@ -445,6 +452,7 @@
         in_specs=[VMEM] * len(operands),
         out_specs=jax.tree.map(lambda _: VMEM, out_shape),
         scratch_shapes=[padded] + list(scratch),
+        compiler_params=pltpu.CompilerParams(vmem_limit_bytes=LIMIT),
     )(*operands)
 
 

time: 170 us -> 129 us (0.76)
  Pallas kernels: 161 us -> 124 us
  local copies, waits for them, and re-layouts: 8.19 us -> 4.65 us
    pallas_call x3, Pallas kernels: 65.3 us -> 43 us  [sweep_call(): pl.pallas_call(kernel, name=name, out_shape=out_shape, in_specs=[VMEM] *...]
    pallas_call x1, Pallas kernels: 16.5 us -> 10 us  [moments(): pl.pallas_call(moments_kernel, name='moments', out_shape=(jax.ShapeDtypeS...]
    unnamed x5, local copies, waits for them, and re-layouts: 8.19 us -> 4.65 us
    pallas_call x2, Pallas kernels: 51.6 us -> 48.2 us  [summed(): pl.pallas_call(functools.partial(sum_kernel, sizes), name='sum_and_halo',...]
    pallas_call x2, Pallas kernels: 16.1 us -> 13 us  [finish(): pl.pallas_call(finish_kernel, name='finish', out_shape=(jax.ShapeDtypeStr...]
    pallas_call x1, Pallas kernels: 11.5 us -> 9.74 us  [halo_of(): pl.pallas_call(functools.partial(halo_kernel, sizes), name='halo', out_sh...]
where the time goes in v3:
time: 129 us
  Pallas kernels  124 us (96%)
  local copies, waits for them, and re-layouts  4.65 us (4%)
    pallas_call x2, Pallas kernels, summed(): pl.pallas_call(functools.partial(sum_kernel, sizes), name='sum_and_halo',...  48.2 us
    pallas_call x3, Pallas kernels, sweep_call(): pl.pallas_call(kernel, name=name, out_shape=out_shape, in_specs=[VMEM] *...  43 us
    pallas_call x2, Pallas kernels, finish(): pl.pallas_call(finish_kernel, name='finish', out_shape=(jax.ShapeDtypeStr...  13 us
    pallas_call x1, Pallas kernels, moments(): pl.pallas_call(moments_kernel, name='moments', out_shape=(jax.ShapeDtypeS...  10 us
    pallas_call x1, Pallas kernels, halo_of(): pl.pallas_call(functools.partial(halo_kernel, sizes), name='halo', out_sh...  9.74 us
    unnamed x5, local copies, waits for them, and re-layouts  4.65 us

profile of v3, /device:TPU:1, one launch (start us, length us, event | category | flops | bytes accessed | tf_op | source)
XLA Modules:
  0.0 129.3 jit_solution(1834809036599542404)
XLA Ops:
  0.6 0.0 copy-start
  0.6 2.1 %copy.10 = bf16[16,8,32,128]{3,0,2,1:T(8,128)(2,1)S(1)} copy(bf16[16,8,32,128]{3,2,1,0:T(8,128)(2,1)} %param.3) | data formatting | bytes 2097152 | tf_op args[1]
  2.7 0.0 copy-done
  2.7 1.4 %copy.9 = bf16[32,8,32,128]{3,0,2,1:T(8,128)(2,1)S(1)} copy(bf16[32,8,32,128]{3,2,1,0:T(8,128)(2,1)S(1)} %copy-done) | data formatting | bytes 4194304 | tf_op args[0]
  4.1 10.0 %moments.1 = (f32[16,9,128]{2,1,0:T(8,128)S(1)}, bf16[1,4096]{1,0:T(2,128)(2,1)S(1)}, bf16[1,4096]{1,0:T(2,128)(2,1)S(1)}) custom-call(bf16[8,32,32,128]{3,2,1,0:T(8,128)(2,1)S(1)} %bitcast.7, bf16[8,32,16,128]{3,2,1,0:T(8,128)(2,1)S(1)} %bitcast.11), custom_call_target="tpu_custom_call" | custom-call | tf_op jit(solution)/shard_map/moments/pallas_call | solution.py:96
  14.1 26.8 %sum_and_halo.2 = (f32[16,9,128]{2,1,0:T(8,128)S(1)}, bf16[32,16,128]{2,1,0:T(8,128)(2,1)S(1)}, bf16[32,16,128]{2,1,0:T(8,128)(2,1)S(1)}, bf16[8,16,128]{2,1,0:T...) custom-call(f32[16,9,128]{2,1,0:T(8,128)S(1)} %get-tuple-element.38.part, ...), custom_call_target="tpu_custom_call" | custom-call | tf_op jit(solution)/shard_map/sum_and_halo/pallas_call | solution.py:257
  40.9 6.5 %finish.2 = (bf16[512,128]{1,0:T(8,128)(2,1)S(1)}, f32[16,128]{1,0:T(8,128)S(1)}, f32[16,32]{1,0:T(8,128)}) custom-call(f32[16,9,128]{2,1,0:T(8,128)S(1)} %get-tuple-element.41.sum_ref), custom_call_target="tpu_custom_call" | custom-call | tf_op jit(solution)/shard_map/finish/pallas_call | solution.py:319
  47.4 15.8 %first_sweep.1 = (bf16[8,32,16,128]{3,2,1,0:T(8,128)(2,1)S(1)}, f32[8,32,16,128]{3,2,1,0:T(8,128)S(1)}, bf16[1,4096]{1,0:T(2,128)(2,1)S(1)}, bf16[1,4096]{1,0:T(2,128)(2,1)S(1)}) custom-call(bf16[8,32,32,128]{3,2,1,0:T(8,128)(2,1)S(1)} %bitcast.8, bf16[512,128]{1,0:T(8,128)(2,1)S(1)} %get-tuple-element.42.m_ref, f32[16,128]{1,0:T(8,128)S(1)} %get-tuple-element.43.b_ref, ...), custom_call_target="tpu_custom_call" | custom-call | tf_op jit(solution)/shard_map/first_sweep/pallas_call | solution.py:448
  63.1 9.7 %halo.1 = (bf16[32,16,128]{2,1,0:T(8,128)(2,1)S(1)}, bf16[32,16,128]{2,1,0:T(8,128)(2,1)S(1)}, bf16[8,16,128]{2,1,0:T(8,128)(2,1)S(1)}, bf16[8,16,128]{2,1,0:T(8...) custom-call(bf16[8,32,16,128]{3,2,1,0:T(8,128)(2,1)S(1)} %get-tuple-element.51.q_ref, ...), custom_call_target="tpu_custom_call" | custom-call | tf_op jit(solution)/shard_map/halo/pallas_call | solution.py:241
  72.9 16.9 %second_sweep.1 = (bf16[8,32,16,128]{3,2,1,0:T(8,128)(2,1)S(1)}, f32[16,9,128]{2,1,0:T(8,128)S(1)}, bf16[1,4096]{1,0:T(2,128)(2,1)S(1)}, bf16[1,4096]{1,0:T(2,128)(2,1)S(1)}) custom-call(bf16[8,32,32,128]{3,2,1,0:T(8,128)(2,1)S(1)} %bitcast.9, f32[8,32,16,128]{3,2,1,0:T(8,128)S(1)} %get-tuple-element.50.scores_ref, ...), custom_call_target="tpu_custom_call" | custom-call | tf_op jit(solution)/shard_map/second_sweep/pallas_call | solution.py:448
  89.8 21.4 %sum_and_halo.3 = (f32[16,9,128]{2,1,0:T(8,128)S(1)}, bf16[32,16,128]{2,1,0:T(8,128)(2,1)S(1)}, bf16[32,16,128]{2,1,0:T(8,128)(2,1)S(1)}, bf16[8,16,128]{2,1,0:T...) custom-call(f32[16,9,128]{2,1,0:T(8,128)S(1)} %get-tuple-element.60.part, ...), custom_call_target="tpu_custom_call" | custom-call | tf_op jit(solution)/shard_map/sum_and_halo/pallas_call | solution.py:257
  111.2 6.5 %finish.3 = (bf16[512,128]{1,0:T(8,128)(2,1)S(1)}, f32[16,128]{1,0:T(8,128)S(1)}, f32[16,32]{1,0:T(8,128)}) custom-call(f32[16,9,128]{2,1,0:T(8,128)S(1)} %get-tuple-element.64.sum_ref), custom_call_target="tpu_custom_call" | custom-call | tf_op jit(solution)/shard_map/finish/pallas_call | solution.py:319
  117.7 10.4 %last_update.1 = bf16[8,32,16,128]{3,2,1,0:T(8,128)(2,1)S(1)} custom-call(bf16[8,32,32,128]{3,2,1,0:T(8,128)(2,1)S(1)} %bitcast.10, bf16[512,128]{1,0:T(8,128)(2,1)S(1)} %get-tuple-element.65.m_ref, f32[16,128]{1,0:T(8,128)S(1)} %get-tuple-element.66.b_ref, bf16[8,32,16,128]{3,2,1,0:T(8,128)(2,1)S(1)} %get-tuple-element.61.q_ref, ...), custom_call_target="tpu_custom_call" | custom-call | tf_op jit(solution)/shard_map/last_update/pallas_call | solution.py:448
  128.1 1.2 copy.6
Async XLA Ops:
  0.6 2.1 %copy-start = (bf16[32,8,32,128]{3,2,1,0:T(8,128)(2,1)S(1)}, bf16[32,8,32,128]{3,2,1,0:T(8,128)(2,1)}, u32[]{:S(2)}) copy-start(bf16[32,8,32,128]{3,2,1,0:T(8,128)(2,1)} %param.2) | copy-start | bytes 6291460

commit v4 on v3

--- a/solution.py
+++ b/solution.py
@@ -37,16 +37,17 @@
     return jnp.concatenate([rows, extra], axis=0)
 
 
-def face_of(q_rows, low_ref, high_ref, step):
+def store_faces(q_ref, low_ref, high_ref):
     side = lax.broadcasted_iota(jnp.int32, (16, LANES), 0)
     lane = lax.broadcasted_iota(jnp.int32, (16, LANES), 1)
     pick = ((side == 0) & (lane == 0)) | ((side == 1) & (lane == LANES - 1))
     pick = jnp.where(pick, 1.0, 0.0).astype(jnp.bfloat16)
-    faces = lax.dot_general(pick, q_rows, NT, preferred_element_type=jnp.float32)
-    width = GROUP * CLASSES
-    where = pl.ds(pl.multiple_of(step * width, width), width)
-    low_ref[:, where] = faces[0:1].astype(jnp.bfloat16)
-    high_ref[:, where] = faces[1:2].astype(jnp.bfloat16)
+    width = q_ref.shape[1] * CLASSES
+    for x in range(q_ref.shape[0]):
+        rows = q_ref[x].reshape(width, LANES)
+        faces = lax.dot_general(pick, rows, NT, preferred_element_type=jnp.float32)
+        low_ref[:, x * width : (x + 1) * width] = faces[0:1].astype(jnp.bfloat16)
+        high_ref[:, x * width : (x + 1) * width] = faces[1:2].astype(jnp.bfloat16)
 
 
 def add_moments(rows, posts, total):
@@ -84,10 +85,10 @@
         rows = [f_ref[x, y + g] for g in range(GROUP)]
         posts = [q_ref[x, y + g] for g in range(GROUP)]
         add_moments(rows, posts, total)
-        face_of(jnp.concatenate(posts, axis=0), low_ref, high_ref, c)
         return carry
 
     lax.fori_loop(0, count_x * per_x, step, 0, unroll=UNROLL)
+    store_faces(q_ref, low_ref, high_ref)
     pack_moments(total, out_ref)
 
 
@@ -152,13 +153,13 @@
 def start_halo(sizes, q_ref, low_ref, high_ref, halo, send, recv):
     last_x, last_y = q_ref.shape[0] - 1, q_ref.shape[1] - 1
     faces = {
+        "gz": (low_ref, high_ref),
         "gx": (q_ref.at[0], q_ref.at[last_x]),
         "gy": (q_ref.at[:, 0], q_ref.at[:, last_y]),
-        "gz": (low_ref, high_ref),
     }
     copies = []
-    for n, (axis, (first, last)) in enumerate(faces.items()):
-        up, down = 2 * n, 2 * n + 1
+    for axis, (first, last) in faces.items():
+        up, down = 2 * AXES.index(axis), 2 * AXES.index(axis) + 1
         copies.append(
             remote(last, halo[up], send.at[up], recv.at[up], beside(sizes, axis, 1))
         )
@@ -295,12 +296,14 @@
         rows.append(jnp.concatenate([unit, shift, spread, jnp.zeros_like(spread)], axis=1))
     diagonal = jnp.ones((CLASSES, LANES), jnp.float32)
     for k in range(FEATS):
-        pivot = jnp.sqrt(rows[k][:, 64 + k : 65 + k])
+        row = rows[k]
+        square = jnp.broadcast_to(row[:, 64 + k : 65 + k], row.shape)
+        inverse = 1.0 / square
+        for i in range(k + 1, FEATS):
+            rows[i] = rows[i] - (row[:, 64 + i : 65 + i] * inverse) * row
+        pivot = jnp.sqrt(square)
         diagonal = jnp.where(lane == k, pivot, diagonal)
-        row = rows[k] * (1.0 / pivot)
-        rows[k] = row
-        for i in range(k + 1, FEATS):
-            rows[i] = rows[i] - row[:, 64 + i : 65 + i] * row
+        rows[k] = row * (1.0 / pivot)
     logdet = jnp.sum(jnp.log(diagonal), axis=1, keepdims=True)
     bias_ref[...] = jnp.broadcast_to(jnp.log(counts / total_weight) - logdet, (CLASSES, LANES))
     for g in range(FEATS):
@@ -401,10 +404,10 @@
         scores_ref[x, pl.ds(y, GROUP)] = scores.reshape(GROUP, CLASSES, LANES)
         q = update(scores, near_of(padded, zlo, zhi, x, y, c))
         out_ref[x, pl.ds(y, GROUP)] = q
-        face_of(q.reshape(GROUP * CLASSES, LANES), low_ref, high_ref, c)
         return carry
 
     lax.fori_loop(0, count_x * per_x, step, 0, unroll=UNROLL)
+    store_faces(out_ref, low_ref, high_ref)
 
 
 def second_kernel(f_ref, scores_ref, q_ref, xlo, xhi, ylo, yhi, zlo, zhi,
@@ -421,10 +424,10 @@
         out_ref[x, pl.ds(y, GROUP)] = q
         rows = [f_ref[x, y + g] for g in range(GROUP)]
         add_moments(rows, [q[g] for g in range(GROUP)], total)
-        face_of(q.reshape(GROUP * CLASSES, LANES), low_ref, high_ref, c)
         return carry
 
     lax.fori_loop(0, count_x * per_x, step, 0, unroll=UNROLL)
+    store_faces(out_ref, low_ref, high_ref)
     pack_moments(total, sum_ref)
 
 

time: 129 us -> 120 us (0.930)
  Pallas kernels: 124 us -> 114 us
    pallas_call x3, Pallas kernels: 43 us -> 38 us  [sweep_call(): pl.pallas_call(kernel, name=name, out_shape=out_shape, in_specs=[VMEM] *...]
    pallas_call x2, Pallas kernels: 13 us -> 8.62 us  [finish(): pl.pallas_call(finish_kernel, name='finish', out_shape=(jax.ShapeDtypeStr...]
where the time goes in v4:
time: 120 us
  Pallas kernels  114 us (95%)
  local copies, waits for them, and re-layouts  4.65 us (4%)
    pallas_call x2, Pallas kernels, summed(): pl.pallas_call(functools.partial(sum_kernel, sizes), name='sum_and_halo',...  47.5 us
    pallas_call x3, Pallas kernels, sweep_call(): pl.pallas_call(kernel, name=name, out_shape=out_shape, in_specs=[VMEM] *...  38 us
    pallas_call x1, Pallas kernels, halo_of(): pl.pallas_call(functools.partial(halo_kernel, sizes), name='halo', out_sh...  10 us
    pallas_call x1, Pallas kernels, moments(): pl.pallas_call(moments_kernel, name='moments', out_shape=(jax.ShapeDtypeS...  10 us
    pallas_call x2, Pallas kernels, finish(): pl.pallas_call(finish_kernel, name='finish', out_shape=(jax.ShapeDtypeStr...  8.62 us
    unnamed x5, local copies, waits for them, and re-layouts  4.65 us

profile of v4, /device:TPU:1, one launch (start us, length us, event | category | flops | bytes accessed | tf_op | source)
XLA Modules:
  0.0 119.6 jit_solution(3350501076921185340)
XLA Ops:
  0.6 0.0 copy-start
  0.6 2.1 %copy.10 = bf16[16,8,32,128]{3,0,2,1:T(8,128)(2,1)S(1)} copy(bf16[16,8,32,128]{3,2,1,0:T(8,128)(2,1)} %param.3) | data formatting | bytes 2097152 | tf_op args[1]
  2.7 0.0 copy-done
  2.7 1.4 %copy.9 = bf16[32,8,32,128]{3,0,2,1:T(8,128)(2,1)S(1)} copy(bf16[32,8,32,128]{3,2,1,0:T(8,128)(2,1)S(1)} %copy-done) | data formatting | bytes 4194304 | tf_op args[0]
  4.1 10.0 %moments.1 = (f32[16,9,128]{2,1,0:T(8,128)S(1)}, bf16[1,4096]{1,0:T(2,128)(2,1)S(1)}, bf16[1,4096]{1,0:T(2,128)(2,1)S(1)}) custom-call(bf16[8,32,32,128]{3,2,1,0:T(8,128)(2,1)S(1)} %bitcast.7, bf16[8,32,16,128]{3,2,1,0:T(8,128)(2,1)S(1)} %bitcast.11), custom_call_target="tpu_custom_call" | custom-call | tf_op jit(solution)/shard_map/moments/pallas_call | solution.py:97
  14.1 26.7 %sum_and_halo.2 = (f32[16,9,128]{2,1,0:T(8,128)S(1)}, bf16[32,16,128]{2,1,0:T(8,128)(2,1)S(1)}, bf16[32,16,128]{2,1,0:T(8,128)(2,1)S(1)}, bf16[8,16,128]{2,1,0:T...) custom-call(f32[16,9,128]{2,1,0:T(8,128)S(1)} %get-tuple-element.38.part, ...), custom_call_target="tpu_custom_call" | custom-call | tf_op jit(solution)/shard_map/sum_and_halo/pallas_call | solution.py:258
  40.8 4.3 %finish.2 = (bf16[512,128]{1,0:T(8,128)(2,1)S(1)}, f32[16,128]{1,0:T(8,128)S(1)}, f32[16,32]{1,0:T(8,128)}) custom-call(f32[16,9,128]{2,1,0:T(8,128)S(1)} %get-tuple-element.41.sum_ref), custom_call_target="tpu_custom_call" | custom-call | tf_op jit(solution)/shard_map/finish/pallas_call | solution.py:322
  45.1 10.8 %first_sweep.1 = (bf16[8,32,16,128]{3,2,1,0:T(8,128)(2,1)S(1)}, f32[8,32,16,128]{3,2,1,0:T(8,128)S(1)}, bf16[1,4096]{1,0:T(2,128)(2,1)S(1)}, bf16[1,4096]{1,0:T(2,128)(2,1)S(1)}) custom-call(bf16[8,32,32,128]{3,2,1,0:T(8,128)(2,1)S(1)} %bitcast.8, bf16[512,128]{1,0:T(8,128)(2,1)S(1)} %get-tuple-element.42.m_ref, f32[16,128]{1,0:T(8,128)S(1)} %get-tuple-element.43.b_ref, ...), custom_call_target="tpu_custom_call" | custom-call | tf_op jit(solution)/shard_map/first_sweep/pallas_call | solution.py:451
  55.9 10.0 %halo.1 = (bf16[32,16,128]{2,1,0:T(8,128)(2,1)S(1)}, bf16[32,16,128]{2,1,0:T(8,128)(2,1)S(1)}, bf16[8,16,128]{2,1,0:T(8,128)(2,1)S(1)}, bf16[8,16,128]{2,1,0:T(8...) custom-call(bf16[8,32,16,128]{3,2,1,0:T(8,128)(2,1)S(1)} %get-tuple-element.51.q_ref, ...), custom_call_target="tpu_custom_call" | custom-call | tf_op jit(solution)/shard_map/halo/pallas_call | solution.py:242
  66.0 16.8 %second_sweep.1 = (bf16[8,32,16,128]{3,2,1,0:T(8,128)(2,1)S(1)}, f32[16,9,128]{2,1,0:T(8,128)S(1)}, bf16[1,4096]{1,0:T(2,128)(2,1)S(1)}, bf16[1,4096]{1,0:T(2,128)(2,1)S(1)}) custom-call(bf16[8,32,32,128]{3,2,1,0:T(8,128)(2,1)S(1)} %bitcast.9, f32[8,32,16,128]{3,2,1,0:T(8,128)S(1)} %get-tuple-element.50.scores_ref, ...), custom_call_target="tpu_custom_call" | custom-call | tf_op jit(solution)/shard_map/second_sweep/pallas_call | solution.py:451
  82.8 20.9 %sum_and_halo.3 = (f32[16,9,128]{2,1,0:T(8,128)S(1)}, bf16[32,16,128]{2,1,0:T(8,128)(2,1)S(1)}, bf16[32,16,128]{2,1,0:T(8,128)(2,1)S(1)}, bf16[8,16,128]{2,1,0:T...) custom-call(f32[16,9,128]{2,1,0:T(8,128)S(1)} %get-tuple-element.60.part, ...), custom_call_target="tpu_custom_call" | custom-call | tf_op jit(solution)/shard_map/sum_and_halo/pallas_call | solution.py:258
  103.7 4.3 %finish.3 = (bf16[512,128]{1,0:T(8,128)(2,1)S(1)}, f32[16,128]{1,0:T(8,128)S(1)}, f32[16,32]{1,0:T(8,128)}) custom-call(f32[16,9,128]{2,1,0:T(8,128)S(1)} %get-tuple-element.64.sum_ref), custom_call_target="tpu_custom_call" | custom-call | tf_op jit(solution)/shard_map/finish/pallas_call | solution.py:322
  108.0 10.4 %last_update.1 = bf16[8,32,16,128]{3,2,1,0:T(8,128)(2,1)S(1)} custom-call(bf16[8,32,32,128]{3,2,1,0:T(8,128)(2,1)S(1)} %bitcast.10, bf16[512,128]{1,0:T(8,128)(2,1)S(1)} %get-tuple-element.65.m_ref, f32[16,128]{1,0:T(8,128)S(1)} %get-tuple-element.66.b_ref, bf16[8,32,16,128]{3,2,1,0:T(8,128)(2,1)S(1)} %get-tuple-element.61.q_ref, ...), custom_call_target="tpu_custom_call" | custom-call | tf_op jit(solution)/shard_map/last_update/pallas_call | solution.py:451
  118.4 1.2 %copy.6 = bf16[16,8,32,128]{3,2,1,0:T(8,128)(2,1)} copy(bf16[16,8,32,128]{3,0,2,1:T(8,128)(2,1)S(1)} %bitcast.14) | data formatting | bytes 2097152
Async XLA Ops:
  0.6 2.1 %copy-start = (bf16[32,8,32,128]{3,2,1,0:T(8,128)(2,1)S(1)}, bf16[32,8,32,128]{3,2,1,0:T(8,128)(2,1)}, u32[]{:S(2)}) copy-start(bf16[32,8,32,128]{3,2,1,0:T(8,128)(2,1)} %param.2) | copy-start | bytes 6291460

commit v5 on v4

--- a/solution.py
+++ b/solution.py
@@ -134,11 +134,15 @@
     return {axis: lax.rem(lax.axis_index(axis) + d + sizes[axis], sizes[axis])}
 
 
-def meet(devices):
+def greet(devices):
     barrier = pltpu.get_barrier_semaphore()
     for device in devices:
         pl.semaphore_signal(barrier, inc=1, device_id=device, device_id_type=MESH)
-    pl.semaphore_wait(barrier, len(devices))
+    return barrier
+
+
+def meet(devices):
+    pl.semaphore_wait(greet(devices), len(devices))
 
 
 def remote(source, target, send, recv, device):
@@ -178,12 +182,6 @@
             @pl.when(lax.axis_index(axis) == edge)
             def _(ref=ref):
                 ref[...] = jnp.zeros_like(ref)
-
-
-def halo_kernel(sizes, q_ref, low_ref, high_ref, *rest):
-    halo, (send, recv) = rest[:6], rest[6:]
-    meet([beside(sizes, axis, d) for axis in AXES for d in (1, -1)])
-    end_halo(sizes, start_halo(sizes, q_ref, low_ref, high_ref, halo, send, recv), halo)
 
 
 def sum_kernel(sizes, part_ref, q_ref, low_ref, high_ref, out_ref, *rest):
@@ -235,19 +233,6 @@
     plane_y = jax.ShapeDtypeStruct((q.shape[0],) + q.shape[2:], q.dtype)
     plane_z = jax.ShapeDtypeStruct(low.shape, low.dtype)
     return (plane_x, plane_x, plane_y, plane_y, plane_z, plane_z)
-
-
-def halo_of(q, low, high):
-    sizes = {axis: lax.axis_size(axis) for axis in AXES}
-    return pl.pallas_call(
-        functools.partial(halo_kernel, sizes),
-        name="halo",
-        out_shape=halo_shapes(q, low),
-        in_specs=[VMEM] * 3,
-        out_specs=(VMEM,) * 6,
-        scratch_shapes=[pltpu.SemaphoreType.DMA((6,)), pltpu.SemaphoreType.DMA((6,))],
-        compiler_params=pltpu.CompilerParams(collective_id=1, vmem_limit_bytes=LIMIT, has_side_effects=True),
-    )(q, low, high)
 
 
 def summed(part, q, low, high):
@@ -392,8 +377,11 @@
     return jnp.concatenate(parts, axis=0)
 
 
-def first_kernel(f_ref, m_ref, b_ref, q_ref, xlo, xhi, ylo, yhi, zlo, zhi,
-                 out_ref, scores_ref, low_ref, high_ref, padded):
+def first_kernel(sizes, f_ref, m_ref, b_ref, q_ref, xlo, xhi, ylo, yhi, zlo, zhi,
+                 out_ref, scores_ref, *rest):
+    halo, (padded, low_ref, high_ref, send, recv) = rest[:6], rest[6:]
+    devices = [beside(sizes, axis, d) for axis in AXES for d in (1, -1)]
+    barrier = greet(devices)
     count_x, count_y = q_ref.shape[0], q_ref.shape[1]
     per_x = count_y // GROUP
     fill_padded(padded, q_ref, xlo, xhi, ylo, yhi)
@@ -408,6 +396,8 @@
 
     lax.fori_loop(0, count_x * per_x, step, 0, unroll=UNROLL)
     store_faces(out_ref, low_ref, high_ref)
+    pl.semaphore_wait(barrier, len(devices))
+    end_halo(sizes, start_halo(sizes, out_ref, low_ref, high_ref, halo, send, recv), halo)
 
 
 def second_kernel(f_ref, scores_ref, q_ref, xlo, xhi, ylo, yhi, zlo, zhi,
@@ -445,7 +435,7 @@
     lax.fori_loop(0, count_x * per_x, step, 0, unroll=UNROLL)
 
 
-def sweep_call(kernel, name, operands, q, out_shape, scratch=()):
+def sweep_call(kernel, name, operands, q, out_shape, scratch=(), **params):
     count_x, count_y = q.shape[0], q.shape[1]
     padded = pltpu.VMEM((count_x + 2, count_y + 2, CLASSES, LANES), jnp.bfloat16)
     return pl.pallas_call(
@@ -455,7 +445,7 @@
         in_specs=[VMEM] * len(operands),
         out_specs=jax.tree.map(lambda _: VMEM, out_shape),
         scratch_shapes=[padded] + list(scratch),
-        compiler_params=pltpu.CompilerParams(vmem_limit_bytes=LIMIT),
+        compiler_params=pltpu.CompilerParams(vmem_limit_bytes=LIMIT, **params),
     )(*operands)
 
 
@@ -471,10 +461,13 @@
     part, low, high = moments(f, q)
     total_sum, halo = summed(part, q, low, high)
     matrix, bias, _ = finish(total_sum)
-    q, scores, low, high = sweep_call(
-        first_kernel, "first_sweep", [f, matrix, bias, q, *halo], q,
-        (state, scores_shape, face, face))
-    halo = halo_of(q, low, high)
+    sizes = {axis: lax.axis_size(axis) for axis in AXES}
+    semaphores = [pltpu.SemaphoreType.DMA((6,)), pltpu.SemaphoreType.DMA((6,))]
+    faces = [pltpu.VMEM(face.shape, face.dtype)] * 2
+    q, scores, *halo = sweep_call(
+        functools.partial(first_kernel, sizes), "first_sweep", [f, matrix, bias, q, *halo], q,
+        (state, scores_shape) + halo_shapes(q, low), faces + semaphores,
+        collective_id=1, has_side_effects=True)
     q, part, low, high = sweep_call(
         second_kernel, "second_sweep", [f, scores, q, *halo], q,
         (state, sums, face, face), [total])

time: 120 us -> 116 us (0.967)
  Pallas kernels: 114 us -> 111 us
    pallas_call x1 -> x0, Pallas kernels: 10 us -> none  [halo_of(): pl.pallas_call(functools.partial(halo_kernel, sizes), name='halo', out_sh...]
    pallas_call x3, Pallas kernels: 38 us -> 44.2 us  [sweep_call(): pl.pallas_call(kernel, name=name, out_shape=out_shape, in_specs=[VMEM] *...]
where the time goes in v5:
time: 116 us
  Pallas kernels  111 us (96%)
  local copies, waits for them, and re-layouts  4.65 us (4%)
    pallas_call x2, Pallas kernels, summed(): pl.pallas_call(functools.partial(sum_kernel, sizes), name='sum_and_halo',...  48.1 us
    pallas_call x3, Pallas kernels, sweep_call(): pl.pallas_call(kernel, name=name, out_shape=out_shape, in_specs=[VMEM] *...  44.2 us
    pallas_call x1, Pallas kernels, moments(): pl.pallas_call(moments_kernel, name='moments', out_shape=(jax.ShapeDtypeS...  10 us
    pallas_call x2, Pallas kernels, finish(): pl.pallas_call(finish_kernel, name='finish', out_shape=(jax.ShapeDtypeStr...  8.62 us
    unnamed x5, local copies, waits for them, and re-layouts  4.65 us

profile of v5, /device:TPU:1, one launch (start us, length us, event | category | flops | bytes accessed | tf_op | source)
XLA Modules:
  0.0 116.2 jit_solution(2937033159475502923)
XLA Ops:
  0.6 0.0 copy-start
  0.6 2.1 %copy.10 = bf16[16,8,32,128]{3,0,2,1:T(8,128)(2,1)S(1)} copy(bf16[16,8,32,128]{3,2,1,0:T(8,128)(2,1)} %param.3) | data formatting | bytes 2097152 | tf_op args[1]
  2.7 0.0 copy-done
  2.7 1.4 %copy.9 = bf16[32,8,32,128]{3,0,2,1:T(8,128)(2,1)S(1)} copy(bf16[32,8,32,128]{3,2,1,0:T(8,128)(2,1)S(1)} %copy-done) | data formatting | bytes 4194304 | tf_op args[0]
  4.1 10.0 %moments.1 = (f32[16,9,128]{2,1,0:T(8,128)S(1)}, bf16[1,4096]{1,0:T(2,128)(2,1)S(1)}, bf16[1,4096]{1,0:T(2,128)(2,1)S(1)}) custom-call(bf16[8,32,32,128]{3,2,1,0:T(8,128)(2,1)S(1)} %bitcast.7, bf16[8,32,16,128]{3,2,1,0:T(8,128)(2,1)S(1)} %bitcast.11), custom_call_target="tpu_custom_call" | custom-call | tf_op jit(solution)/shard_map/moments/pallas_call | solution.py:97
  14.1 26.7 %sum_and_halo.2 = (f32[16,9,128]{2,1,0:T(8,128)S(1)}, bf16[32,16,128]{2,1,0:T(8,128)(2,1)S(1)}, bf16[32,16,128]{2,1,0:T(8,128)(2,1)S(1)}, bf16[8,16,128]{2,1,0:T...) custom-call(f32[16,9,128]{2,1,0:T(8,128)S(1)} %get-tuple-element.36.part, ...), custom_call_target="tpu_custom_call" | custom-call | tf_op jit(solution)/shard_map/sum_and_halo/pallas_call | solution.py:243
  40.8 4.3 %finish.2 = (bf16[512,128]{1,0:T(8,128)(2,1)S(1)}, f32[16,128]{1,0:T(8,128)S(1)}, f32[16,32]{1,0:T(8,128)}) custom-call(f32[16,9,128]{2,1,0:T(8,128)S(1)} %get-tuple-element.39.sum_ref), custom_call_target="tpu_custom_call" | custom-call | tf_op jit(solution)/shard_map/finish/pallas_call | solution.py:307
  45.1 17.0 %first_sweep.1 = (bf16[8,32,16,128]{3,2,1,0:T(8,128)(2,1)S(1)}, f32[8,32,16,128]{3,2,1,0:T(8,128)S(1)}, bf16[32,16,128]{2,1,0:T(8,128)(2,1)S(1)}, bf16[32,16,128...) custom-call(bf16[8,32,32,128]{3,2,1,0:T(8,128)(2,1)S(1)} %bitcast.8,, ...), custom_call_target="tpu_custom_call" | custom-call | tf_op jit(solution)/shard_map/first_sweep/pallas_call | solution.py:441
  62.1 16.8 %second_sweep.1 = (bf16[8,32,16,128]{3,2,1,0:T(8,128)(2,1)S(1)}, f32[16,9,128]{2,1,0:T(8,128)S(1)}, bf16[1,4096]{1,0:T(2,128)(2,1)S(1)}, bf16[1,4096]{1,0:T(2,128)(2,1)S(1)}) custom-call(bf16[8,32,32,128]{3,2,1,0:T(8,128)(2,1)S(1)} %bitcast.9, f32[8,32,16,128]{3,2,1,0:T(8,128)S(1)} %get-tuple-element.48.scores_ref, ...), custom_call_target="tpu_custom_call" | custom-call | tf_op jit(solution)/shard_map/second_sweep/pallas_call | solution.py:441
  78.8 21.4 %sum_and_halo.3 = (f32[16,9,128]{2,1,0:T(8,128)S(1)}, bf16[32,16,128]{2,1,0:T(8,128)(2,1)S(1)}, bf16[32,16,128]{2,1,0:T(8,128)(2,1)S(1)}, bf16[8,16,128]{2,1,0:T...) custom-call(f32[16,9,128]{2,1,0:T(8,128)S(1)} %get-tuple-element.56.part, ...), custom_call_target="tpu_custom_call" | custom-call | tf_op jit(solution)/shard_map/sum_and_halo/pallas_call | solution.py:243
  100.3 4.3 %finish.3 = (bf16[512,128]{1,0:T(8,128)(2,1)S(1)}, f32[16,128]{1,0:T(8,128)S(1)}, f32[16,32]{1,0:T(8,128)}) custom-call(f32[16,9,128]{2,1,0:T(8,128)S(1)} %get-tuple-element.60.sum_ref), custom_call_target="tpu_custom_call" | custom-call | tf_op jit(solution)/shard_map/finish/pallas_call | solution.py:307
  104.6 10.4 %last_update.1 = bf16[8,32,16,128]{3,2,1,0:T(8,128)(2,1)S(1)} custom-call(bf16[8,32,32,128]{3,2,1,0:T(8,128)(2,1)S(1)} %bitcast.10, bf16[512,128]{1,0:T(8,128)(2,1)S(1)} %get-tuple-element.61.m_ref, f32[16,128]{1,0:T(8,128)S(1)} %get-tuple-element.62.b_ref, bf16[8,32,16,128]{3,2,1,0:T(8,128)(2,1)S(1)} %get-tuple-element.57.q_ref, ...), custom_call_target="tpu_custom_call" | custom-call | tf_op jit(solution)/shard_map/last_update/pallas_call | solution.py:441
  115.0 1.2 %copy.6 = bf16[16,8,32,128]{3,2,1,0:T(8,128)(2,1)} copy(bf16[16,8,32,128]{3,0,2,1:T(8,128)(2,1)S(1)} %bitcast.14) | data formatting | bytes 2097152
Async XLA Ops:
  0.6 2.1 %copy-start = (bf16[32,8,32,128]{3,2,1,0:T(8,128)(2,1)S(1)}, bf16[32,8,32,128]{3,2,1,0:T(8,128)(2,1)}, u32[]{:S(2)}) copy-start(bf16[32,8,32,128]{3,2,1,0:T(8,128)(2,1)} %param.2) | copy-start | bytes 6291460
